TPU v7x, 512 devices: a whole 4x4x16 slice. The times are simulated.
512 devices in a mesh: segment: 4 (over x), expert: 64 (over y, z), dp: 2 (over core).
Axes of the slice: x: 4, y: 4, z: 16, core: 2. Of those that a mesh axis runs over, the one named last changes fastest.
Arguments:
- act_in: bfloat16 [4, 14336, 2048], P('segment', ('expert', 'dp')), may hold values from -6 to 6
- stash_in: bfloat16 [4, 14336, 2048], P('segment', ('expert', 'dp')), may hold values from -6 to 6
- grad_in: bfloat16 [4, 14336, 2048], P('segment', ('expert', 'dp')), may hold values from -6 to 6
- route_a: int32 [4, 14336, 2], P('segment', ('expert', 'dp')), may hold values from 0 to 31, all different within a row; in each aligned block of 112 rows (0 to 111, 112 to 223, ..., all dimensions but the last counted through in order) at most 8 rows name the same one
- route_b: int32 [4, 14336, 2], P('segment', ('expert', 'dp')), may hold values from 0 to 31, all different within a row; in each aligned block of 112 rows (0 to 111, 112 to 223, ..., all dimensions but the last counted through in order) at most 8 rows name the same one
- norm_gain: float32 [4, 2048], P('segment'), may hold values from 0.5 to 1.5
- router: bfloat16 [4, 32, 2048], P('segment'), may hold values from -0.5 to 0.5
- gate_weight: bfloat16 [4, 64, 352, 2048], P('segment', 'expert', 'dp'), may hold values from -0.125 to 0.125
- up_weight: bfloat16 [4, 64, 352, 2048], P('segment', 'expert', 'dp'), may hold values from -0.125 to 0.125
- down_weight: bfloat16 [4, 64, 352, 2048], P('segment', 'expert', 'dp'), may hold values from -0.21875 to 0.21875
Outputs:
- next_act: bfloat16 [4, 14336, 2048], P('segment', ('expert', 'dp'))
- prev_grad: bfloat16 [4, 14336, 2048], P('segment', ('expert', 'dp'))
- router_grad: float32 [4, 32, 2048], P('segment')
- gain_grad: float32 [4, 2048], P('segment')
Inputs may be any that keep to these rules, and one draw needn't show every extreme that they name: `route_a`: each row names two different experts. In each aligned block of 112 rows (the tokens of one device) no expert is named more than 8 times, a bound that some block reaches in every draw. `route_b`: as route_a.
All inputs are finite; a program needn't handle non-finite values.
Results may differ from a plain program's by a relative error of at most 0.011.
Values may be sent and summed in bfloat16 or wider, within the bound.
A program may use at most 64 MiB of HBM per device.

v0:
```python
import jax
import jax.numpy as jnp
from jax import lax
from jax.sharding import PartitionSpec as P

EPS = 1e-06


def partner_2(shard, axis, stride):
    return lax.ppermute(shard, axis, [(i, i ^ 1 << stride) for i in range(lax.axis_size(axis))])


def from_behind(value, axis, steps):
    count = lax.axis_size(axis)
    pairs = [(source, (source + steps) % count) for source in range(count)]
    return lax.ppermute(value, axis, pairs)


def order_halves(own_part, far_part, parity):
    low_half = jnp.where(parity == 0, own_part, far_part)
    high_half = jnp.where(parity == 0, far_part, own_part)
    return jnp.stack([low_half, high_half])


def prepare(x_block, route, gain, router_w):
    x_float = x_block.astype(jnp.float32)
    inv_rms = lax.rsqrt(jnp.mean(x_float * x_float, -1, keepdims=True) + EPS)
    normed = (x_float * inv_rms * gain[None, :]).astype(jnp.bfloat16)
    logits = jnp.einsum("td,ed->te", normed, router_w, preferred_element_type=jnp.float32)
    chosen_mask = route[:, :, None] == jnp.arange(router_w.shape[0], dtype=jnp.int32)[None, None, :]
    chosen = jnp.sum(jnp.where(chosen_mask, logits[:, None, :], 0.0), -1)
    weight_one = jax.nn.sigmoid(chosen[:, 0] - chosen[:, 1])
    weight_two = jax.nn.sigmoid(chosen[:, 1] - chosen[:, 0])
    return (x_float, inv_rms, normed, chosen_mask, weight_one, weight_two)


def route_slots(route, experts, capacity, owners, offset):
    expert_ids = route.reshape(-1)
    onehot = (expert_ids[:, None] == jnp.arange(experts, dtype=jnp.int32)[None, :]).astype(
        jnp.int32
    )
    rank = jnp.sum(jnp.cumsum(onehot, axis=0) * onehot, -1) - 1
    position = (2 * expert_ids + (rank + offset) % 2) * capacity + rank // 2
    pair_count = expert_ids.shape[0]
    slot_pair = jnp.full((owners * capacity,), pair_count, jnp.int32)
    slot_pair = slot_pair.at[position].set(jnp.arange(pair_count, dtype=jnp.int32))
    return (position, slot_pair)


def pad_rows(rows):
    return jnp.concatenate([rows, jnp.zeros((1, rows.shape[1]), rows.dtype)], 0)


def body(
    act_in,
    stash_in,
    grad_in,
    route_a,
    route_b,
    norm_gain,
    router,
    gate_weight,
    up_weight,
    down_weight,
):
    parity = lax.axis_index("expert") % 2
    quarters = (gate_weight[0, 0], up_weight[0, 0], down_weight[0, 0])
    halves = (
        lax.all_gather(quarters[0], "dp", axis=0, tiled=True),
        lax.all_gather(quarters[1], "dp", axis=0, tiled=True),
        lax.all_gather(quarters[2], "dp", axis=0, tiled=True),
    )
    partner = partner_2((halves[0], halves[1], halves[2]), "expert", 0)
    weights = tuple((order_halves(halves[which], partner[which], parity) for which in range(3)))
    gate_full, up_full, down_full = weights
    gain = norm_gain[0]
    router_w = router[0]
    experts = router_w.shape[0]
    width = act_in.shape[2]
    tokens = act_in.shape[1]
    owners = lax.axis_size("expert")
    most_rows = 2 * min(tokens // experts + 1, tokens // 2)
    capacity = (most_rows + 1) // 2

    def expert_forward(block_rows):
        flat_rows = block_rows.reshape(-1, width)
        gate_val = jnp.einsum(
            "rd,phd->rph", flat_rows, gate_full, preferred_element_type=jnp.float32
        )
        up_val = jnp.einsum("rd,phd->rph", flat_rows, up_full, preferred_element_type=jnp.float32)
        hidden = (jax.nn.silu(gate_val) * up_val).astype(jnp.bfloat16)
        output = jnp.einsum("rph,phd->rd", hidden, down_full, preferred_element_type=jnp.float32)
        return (output.astype(jnp.bfloat16).reshape(block_rows.shape), gate_val, up_val)

    x_float, inv_rms, normed, chosen_mask, weight_one, weight_two = prepare(
        act_in[0], route_a[0], gain, router_w
    )
    position, slot_pair = route_slots(route_a[0], experts, capacity, owners, parity)
    send_rows = jnp.take(pad_rows(normed), slot_pair // 2, axis=0).reshape(owners, capacity, width)
    output, gate_val, up_val = expert_forward(
        lax.all_to_all(send_rows, "expert", split_axis=0, concat_axis=0, tiled=True)
    )
    returned = lax.all_to_all(output, "expert", split_axis=0, concat_axis=0, tiled=True)
    pair_out = (
        jnp.take(returned.reshape(-1, width), position, axis=0)
        .reshape(tokens, 2, width)
        .astype(jnp.float32)
    )
    mixed = x_float + weight_one[:, None] * pair_out[:, 0] + weight_two[:, None] * pair_out[:, 1]
    next_act = from_behind(mixed.astype(jnp.bfloat16), "segment", 1)
    x_float, inv_rms, normed, chosen_mask, weight_one, weight_two = prepare(
        stash_in[0], route_b[0], gain, router_w
    )
    position, slot_pair = route_slots(route_b[0], experts, capacity, owners, parity)
    send_rows = jnp.take(pad_rows(normed), slot_pair // 2, axis=0).reshape(owners, capacity, width)
    received = lax.all_to_all(send_rows, "expert", split_axis=0, concat_axis=0, tiled=True)
    expert_out, gate_val, up_val = expert_forward(received)
    returned = lax.all_to_all(expert_out, "expert", split_axis=0, concat_axis=0, tiled=True)
    pair_out = (
        jnp.take(returned.reshape(-1, width), position, axis=0)
        .reshape(tokens, 2, width)
        .astype(jnp.float32)
    )
    out_grad = grad_in[0].astype(jnp.float32)
    dot_one = jnp.sum(out_grad * pair_out[:, 0], -1)
    dot_two = jnp.sum(out_grad * pair_out[:, 1], -1)
    logit_grad = weight_one * weight_two * (dot_one - dot_two)
    signs = chosen_mask[:, 0].astype(jnp.float32) - chosen_mask[:, 1].astype(jnp.float32)
    dlogits = (logit_grad[:, None] * signs).astype(jnp.bfloat16)
    pair_grad = jnp.stack(
        [weight_one[:, None] * out_grad, weight_two[:, None] * out_grad], 1
    ).astype(jnp.bfloat16)
    send_grads = jnp.take(
        pad_rows(pair_grad.reshape(tokens * 2, width)), slot_pair, axis=0
    ).reshape(owners, capacity, width)
    grad_rows = lax.all_to_all(
        send_grads, "expert", split_axis=0, concat_axis=0, tiled=True
    ).reshape(-1, width)
    grad_hidden = jnp.einsum(
        "rd,phd->rph", grad_rows, down_full, preferred_element_type=jnp.float32
    )
    sigma = jax.nn.sigmoid(gate_val)
    grad_gate = (grad_hidden * up_val * sigma * (1.0 + gate_val * (1.0 - sigma))).astype(
        jnp.bfloat16
    )
    grad_up = (grad_hidden * gate_val * sigma).astype(jnp.bfloat16)
    grad_normed_rows = jnp.einsum(
        "rph,phd->rd", grad_gate, gate_full, preferred_element_type=jnp.float32
    )
    grad_normed_rows = grad_normed_rows + jnp.einsum(
        "rph,phd->rd", grad_up, up_full, preferred_element_type=jnp.float32
    )
    grad_normed_rows = grad_normed_rows.astype(jnp.bfloat16).reshape(owners, capacity, width)
    grad_back = lax.all_to_all(grad_normed_rows, "expert", split_axis=0, concat_axis=0, tiled=True)
    pair_back = (
        jnp.take(grad_back.reshape(-1, width), position, axis=0)
        .reshape(tokens, 2, width)
        .astype(jnp.float32)
    )
    dnormed = (
        pair_back[:, 0]
        + pair_back[:, 1]
        + jnp.dot(dlogits, router_w, preferred_element_type=jnp.float32)
    )
    router_term = jnp.einsum("te,td->ed", dlogits, normed, preferred_element_type=jnp.float32)
    gain_term = jnp.sum(dnormed * x_float * inv_rms, 0)
    router_sum, gain_sum = lax.psum((router_term, gain_term), ("expert", "dp"))
    blocks = lax.axis_size("expert") * lax.axis_size("dp")
    dxn = dnormed * gain[None, :]
    input_grad = (
        out_grad + inv_rms * dxn - x_float * inv_rms**3 * jnp.mean(dxn * x_float, -1, keepdims=True)
    )
    prev_grad = from_behind(input_grad.astype(jnp.bfloat16), "segment", -1)
    return (next_act[None], prev_grad[None], (router_sum / blocks)[None], (gain_sum / blocks)[None])


def solution(mesh):
    in_specs = (
        P("segment", ("expert", "dp"), None),
        P("segment", ("expert", "dp"), None),
        P("segment", ("expert", "dp"), None),
        P("segment", ("expert", "dp"), None),
        P("segment", ("expert", "dp"), None),
        P("segment", None),
        P("segment", None, None),
        P("segment", "expert", "dp", None),
        P("segment", "expert", "dp", None),
        P("segment", "expert", "dp", None),
    )
    out_specs = (
        P("segment", ("expert", "dp"), None),
        P("segment", ("expert", "dp"), None),
        P("segment", None, None),
        P("segment", None),
    )
    return jax.shard_map(body, mesh=mesh, in_specs=in_specs, out_specs=out_specs, check_vma=False)
```

profile of v0, /device:TPU:1, one launch (start us, length us, event | category | flops | bytes accessed | tf_op | source)
XLA Modules:
  0.0 1096.4 jit_solution(4540719086788931568)
XLA Ops:
  16.1 1.3 scatter_custom_fusion.1
  17.4 1.4 gather_fusion.3
  19.0 1.3 reshape.523
  20.2 19.3 %all-to-all-start.3 = ((bf16[64,4,2048]{2,1,0:T(4,128)(2,1)}), bf16[64,4,2048]{2,1,0:T(4,128)(2,1)S(1)}, u32[]{:S(2)}, u32[]{:S(2)}) async-start(bf16[64,4,2048]{2,1,0:T(4,128)(2,1)} %reshape.523), calls=%async_computation.3 | async-start | bytes 2097152 | tf_op jit(solution)/shard_map/all_to_all | solution.py:116
  40.3 2.9 collective-permute-start
  43.2 17.3 %all-gather.9.cloned.1.call-done = bf16[1,1,352,2048]{3,2,1,0:T(8,128)(2,1)} async-done(((bf16[1,1,176,2048]{3,2,1,0:T(8,128)(2,1)}), bf16[1,1,352,2048]{3,2,1,0:T(8,128)(2,1)}) %all-gather.9.cloned.1.call-update) | async-done | bytes 1441808 | tf_op jit(solution)/shard_map/all_gather | solution.py:70
  60.5 2.2 collective-permute-start.1
  62.7 21.4 %all-gather.11.cloned.1.call-done = bf16[1,1,352,2048]{3,2,1,0:T(8,128)(2,1)} async-done(((bf16[1,1,176,2048]{3,2,1,0:T(8,128)(2,1)}), bf16[1,1,352,2048]{3,2,1,0:T(8,128)(2,1)}) %all-gather.11.cloned.1.call-update) | async-done | bytes 1441808 | tf_op jit(solution)/shard_map/all_gather | solution.py:71
  84.1 2.2 collective-permute-start.2
  86.3 30.3 %collective-permute-done = bf16[352,2048]{1,0:T(8,128)(2,1)} collective-permute-done((bf16[352,2048]{1,0:T(8,128)(2,1)}, bf16[352,2048]{1,0:T(8,128)(2,1)}, u32[]{:S(2)}, u32[]{:S(2)}) %collective-permute-start) | collective-permute-done | bytes 1441824 | tf_op jit(solution)/shard_map/ppermute | solution.py:10
  116.5 3.1 select_bitcast_fusion.5
  119.6 27.8 %collective-permute-done.1 = bf16[352,2048]{1,0:T(8,128)(2,1)} collective-permute-done((bf16[352,2048]{1,0:T(8,128)(2,1)}, bf16[352,2048]{1,0:T(8,128)(2,1)}, u32[]{:S(2)}, u32[]{:S(2)}) %collective-permute-start.1) | collective-permute-done | bytes 1441824 | tf_op jit(solution)/shard_map/ppermute | solution.py:10
  147.4 3.2 select_bitcast_fusion.3
  150.6 27.7 %collective-permute-done.2 = bf16[352,2048]{1,0:T(8,128)(2,1)} collective-permute-done((bf16[352,2048]{1,0:T(8,128)(2,1)}, bf16[352,2048]{1,0:T(8,128)(2,1)}, u32[]{:S(2)}, u32[]{:S(2)}) %collective-permute-start.2) | collective-permute-done | bytes 1441824 | tf_op jit(solution)/shard_map/ppermute | solution.py:10
  178.3 3.2 select_bitcast_fusion.1
  182.6 2.8 fusion.45
  190.1 15.0 %all-to-all-start.5 = ((bf16[64,4,2048]{2,1,0:T(4,128)(2,1)}), bf16[64,4,2048]{2,1,0:T(4,128)(2,1)S(1)}, u32[]{:S(2)}, u32[]{:S(2)}) async-start(bf16[64,4,2048]{2,1,0:T(4,128)(2,1)} %reshape.527), calls=%async_computation.5 | async-start | bytes 2097152 | tf_op jit(solution)/shard_map/all_to_all | solution.py:118
  205.7 49.7 %all-to-all-done.5 = bf16[64,4,2048]{2,1,0:T(4,128)(2,1)S(1)} async-done(((bf16[64,4,2048]{2,1,0:T(4,128)(2,1)}), bf16[64,4,2048]{2,1,0:T(4,128)(2,1)S(1)}, u32[]{:S(2)}, u32[]{:S(2)}) %all-to-all-start.5) | async-done | bytes 1048608 | tf_op jit(solution)/shard_map/all_to_all | solution.py:118
  255.7 1.3 gather_fusion.5
  256.9 1.4 select_convert_fusion
  258.3 2.4 reshape.537
  260.7 1.4 fusion.96
  265.0 1.4 gather_fusion
  267.4 60.5 %all_to_all.30 = bf16[64,4,2048]{2,1,0:T(4,128)(2,1)S(1)} all-to-all(bf16[64,4,2048]{2,1,0:T(4,128)(2,1)S(1)} %broadcast_select_fusion.2), channel_id=1, replica_groups=mesh['segment'=4,'expert'=64,'dp'=2] {'expert'}, dimensions={0} | all-to-all | bytes 2097152 | tf_op jit(solution)/shard_map/all_to_all | solution.py:136
  329.0 2.8 fusion.42
  335.0 1.3 reshape.525
  336.2 10.1 all-to-all-start.4
  346.4 1.4 scatter_custom_fusion
  347.8 48.8 %all-to-all-done.4 = bf16[64,4,2048]{2,1,0:T(4,128)(2,1)S(1)} async-done(((bf16[64,4,2048]{2,1,0:T(4,128)(2,1)}), bf16[64,4,2048]{2,1,0:T(4,128)(2,1)S(1)}, u32[]{:S(2)}, u32[]{:S(2)}) %all-to-all-start.4) | async-done | bytes 1048608 | tf_op jit(solution)/shard_map/all_to_all | solution.py:154
  398.2 1.5 select_convert_fusion.1
  399.7 2.4 reshape.536
  402.1 1.4 fusion.95
  405.9 1.4 gather_fusion.1
  407.8 60.2 %all_to_all.31 = bf16[64,4,2048]{2,1,0:T(4,128)(2,1)S(1)} all-to-all(bf16[64,4,2048]{2,1,0:T(4,128)(2,1)S(1)} %reshape.516), channel_id=1, replica_groups=mesh['segment'=4,'expert'=64,'dp'=2] {'expert'}, dimensions={0} | all-to-all | bytes 2097152 | tf_op jit(solution)/shard_map/all_to_all | solution.py:101
  469.2 4.0 fusion.44
  473.3 7.1 fusion.2
  480.3 2.2 reshape.518
  482.6 10.2 all-to-all-start.1
  494.4 4.4 collective-permute-start.4
  498.8 44.7 %all-to-all-done.1 = bf16[64,4,2048]{2,1,0:T(4,128)(2,1)S(1)} async-done(((bf16[64,4,2048]{2,1,0:T(4,128)(2,1)}), bf16[64,4,2048]{2,1,0:T(4,128)(2,1)S(1)}, u32[]{:S(2)}, u32[]{:S(2)}) %all-to-all-start.1) | async-done | bytes 1048608 | tf_op jit(solution)/shard_map/all_to_all | solution.py:103
  545.0 1.5 select_convert_fusion.2
  546.5 2.4 reshape.531
  548.9 1.4 fusion.97
  551.2 3.1 collective-permute-start.3
  554.4 278.7 %all-reduce.7.cloned.1.call-done = f32[32,2048]{1,0:T(8,128)} async-done(((f32[32,2048]{1,0:T(8,128)}), f32[32,2048]{1,0:T(8,128)}) %all-reduce.7.cloned.1.call-update) | async-done | bytes 262160 | tf_op jit(solution)/shard_map/psum | solution.py:167
  833.1 1.7 multiply_bitcast_fusion
  834.8 251.6 %psum.15 = f32[2048]{0:T(1024)S(1)} all-reduce(f32[2048]{0:T(1024)S(1)} %get-tuple-element.6), channel_id=1, replica_groups=mesh['segment'=4,'expert'=64,'dp'=2] {'expert','dp'}, use_global_device_ids=true, to_apply=%region_17.20 | all-reduce | flops 2048 | bytes 16384 | tf_op jit(solution)/shard_map/psum | solution.py:167
  1087.8 1.8 copy.74
  (156 shorter events, 35.1 us)
Async XLA Ops:
  7.2 198.1 %copy-start = (bf16[1,32,2048]{2,1,0:T(8,128)(2,1)S(1)}, bf16[1,32,2048]{2,1,0:T(8,128)(2,1)}, u32[]{:S(2)}) copy-start(bf16[1,32,2048]{2,1,0:T(8,128)(2,1)} %param.20) | copy-start | bytes 393220
  7.2 7.2 copy-start.2
  7.2 7.4 copy-start.1
  7.2 8.1 copy-start.20
  7.2 33.0 %all-gather.7.cloned.1.call-start = ((), (), s32[]{:S(2)}) async-start(), calls=%async_computation.7 | async-start | bytes 2162688 | tf_op jit(solution)/shard_map/all_gather | solution.py:69
  7.9 52.6 %all-gather.9.cloned.1.call-start = ((), (), s32[]{:S(2)}) async-start(), calls=%async_computation.8 | async-start | bytes 2162688 | tf_op jit(solution)/shard_map/all_gather | solution.py:70
  20.2 161.3 %all-to-all-start.3 = ((bf16[64,4,2048]{2,1,0:T(4,128)(2,1)}), bf16[64,4,2048]{2,1,0:T(4,128)(2,1)S(1)}, u32[]{:S(2)}, u32[]{:S(2)}) async-start(bf16[64,4,2048]{2,1,0:T(4,128)(2,1)} %reshape.523), calls=%async_computation.3 | async-start | bytes 2097152 | tf_op jit(solution)/shard_map/all_to_all | solution.py:116
  39.5 44.6 %all-gather.11.cloned.1.call-start = ((), (), s32[]{:S(2)}) async-start(), calls=%async_computation.9 | async-start | bytes 2162688 | tf_op jit(solution)/shard_map/all_gather | solution.py:71
  40.3 76.3 %collective-permute-start = (bf16[352,2048]{1,0:T(8,128)(2,1)}, bf16[352,2048]{1,0:T(8,128)(2,1)}, u32[]{:S(2)}, u32[]{:S(2)}) collective-permute-start(bf16[352,2048]{1,0:T(8,128)(2,1)} %bitcast.208), channel_id=1, source_target_pairs={{0,2},{2,0},{4,6},{6,4},{8,10},{10,8},{12,14},{14,12},{16,18},{18,... | collective-permute-start | bytes 4325384 | tf_op jit(solution)/shard_map/ppermute | solution.py:10
  60.5 86.9 %collective-permute-start.1 = (bf16[352,2048]{1,0:T(8,128)(2,1)}, bf16[352,2048]{1,0:T(8,128)(2,1)}, u32[]{:S(2)}, u32[]{:S(2)}) collective-permute-start(bf16[352,2048]{1,0:T(8,128)(2,1)} %bitcast.209), channel_id=1, source_target_pairs={{0,2},{2,0},{4,6},{6,4},{8,10},{10,8},{12,14},{14,12},{16,18},{18,... | collective-permute-start | bytes 4325384 | tf_op jit(solution)/shard_map/ppermute | solution.py:10
  84.1 94.3 %collective-permute-start.2 = (bf16[352,2048]{1,0:T(8,128)(2,1)}, bf16[352,2048]{1,0:T(8,128)(2,1)}, u32[]{:S(2)}, u32[]{:S(2)}) collective-permute-start(bf16[352,2048]{1,0:T(8,128)(2,1)} %bitcast.210), channel_id=1, source_target_pairs={{0,2},{2,0},{4,6},{6,4},{8,10},{10,8},{12,14},{14,12},{16,18},{18,... | collective-permute-start | bytes 4325384 | tf_op jit(solution)/shard_map/ppermute | solution.py:10
  86.3 61.2 %copy-start.17 = (bf16[1,1,352,2048]{3,2,1,0:T(8,128)(2,1)S(1)}, bf16[1,1,352,2048]{3,2,1,0:T(8,128)(2,1)}, u32[]{:S(2)}) copy-start(bf16[1,1,352,2048]{3,2,1,0:T(8,128)(2,1)} %all-gather.9.cloned.1.call-done) | copy-start | bytes 4325380
  119.6 62.9 %copy-start.6 = (bf16[1,352,2048]{2,1,0:T(8,128)(2,1)}, bf16[1,352,2048]{2,1,0:T(8,128)(2,1)S(1)}, u32[]{:S(2)}) copy-start(bf16[1,352,2048]{2,1,0:T(8,128)(2,1)S(1)} %get-tuple-element.21) | copy-start | bytes 4325380
  119.6 58.7 %copy-start.18 = (bf16[1,1,352,2048]{3,2,1,0:T(8,128)(2,1)S(1)}, bf16[1,1,352,2048]{3,2,1,0:T(8,128)(2,1)}, u32[]{:S(2)}) copy-start(bf16[1,1,352,2048]{3,2,1,0:T(8,128)(2,1)} %all-gather.11.cloned.1.call-done) | copy-start | bytes 4325380
  182.6 2.8 copy-start.10
  182.6 2.8 copy-start.12
  182.6 2.8 copy-start.19
  185.4 1.0 copy-start.25
  185.4 1.6 copy-start.14
  185.4 2.3 copy-start.16
  186.4 2.4 copy-start.27
  190.1 15.5 %copy-start.21 = (s32[1,112,2]{1,2,0:T(2,128)S(1)}, s32[1,112,2]{1,2,0:T(2,128)}, u32[]{:S(2)}) copy-start(s32[1,112,2]{1,2,0:T(2,128)} %param.18) | copy-start | bytes 2692
  190.1 65.3 %all-to-all-start.5 = ((bf16[64,4,2048]{2,1,0:T(4,128)(2,1)}), bf16[64,4,2048]{2,1,0:T(4,128)(2,1)S(1)}, u32[]{:S(2)}, u32[]{:S(2)}) async-start(bf16[64,4,2048]{2,1,0:T(4,128)(2,1)} %reshape.527), calls=%async_computation.5 | async-start | bytes 2097152 | tf_op jit(solution)/shard_map/all_to_all | solution.py:118
  260.7 1.4 copy-start.4
  267.4 61.6 %copy-start.15 = (bf16[1,352,2048]{2,1,0:T(8,128)(2,1)S(1)}, bf16[1,352,2048]{2,1,0:T(8,128)(2,1)}, u32[]{:S(2)}) copy-start(bf16[1,352,2048]{2,1,0:T(8,128)(2,1)} %get-tuple-element.25) | copy-start | bytes 4325380
  329.0 2.8 copy-start.11
  329.0 2.8 copy-start.13
  329.0 2.8 copy-start.26
  331.8 1.4 copy-start.7
  331.8 1.8 copy-start.9
  331.9 2.0 copy-start.28
  336.2 60.4 %all-to-all-start.4 = ((bf16[64,4,2048]{2,1,0:T(4,128)(2,1)}), bf16[64,4,2048]{2,1,0:T(4,128)(2,1)S(1)}, u32[]{:S(2)}, u32[]{:S(2)}) async-start(bf16[64,4,2048]{2,1,0:T(4,128)(2,1)} %reshape.525), calls=%async_computation.4 | async-start | bytes 2097152 | tf_op jit(solution)/shard_map/all_to_all | solution.py:154
  402.1 1.5 copy-start.24
  403.5 1.0 copy-start.3
  403.5 1.1 copy-start.5
  403.5 1.1 copy-start.23
  469.2 4.0 copy-start.8
  482.6 10.7 copy-start.22
  482.6 60.9 %all-to-all-start.1 = ((bf16[64,4,2048]{2,1,0:T(4,128)(2,1)}), bf16[64,4,2048]{2,1,0:T(4,128)(2,1)S(1)}, u32[]{:S(2)}, u32[]{:S(2)}) async-start(bf16[64,4,2048]{2,1,0:T(4,128)(2,1)} %reshape.518), calls=%async_computation.1 | async-start | bytes 2097152 | tf_op jit(solution)/shard_map/all_to_all | solution.py:103
  492.8 340.3 %all-reduce.7.cloned.1.call-start = ((), (), s32[]{:S(2)}) async-start(), calls=%async_computation.6 | async-start | bytes 524288 | tf_op jit(solution)/shard_map/psum | solution.py:167
  494.4 592.7 %collective-permute-start.4 = (bf16[112,2048]{1,0:T(8,128)(2,1)}, bf16[112,2048]{1,0:T(8,128)(2,1)}, u32[]{:S(2)}, u32[]{:S(2)}) collective-permute-start(bf16[112,2048]{1,0:T(8,128)(2,1)} %get-tuple-element.35), channel_id=1, source_target_pairs={{0,384},{128,0},{256,128},{384,256},{1,385},{129,1},{257,129},{385... | collective-permute-start | bytes 1376264 | tf_op jit(solution)/shard_map/ppermute | solution.py:16
  551.2 535.8 %collective-permute-start.3 = (bf16[112,2048]{1,0:T(8,128)(2,1)S(1)}, bf16[112,2048]{1,0:T(8,128)(2,1)S(1)}, u32[]{:S(2)}, u32[]{:S(2)}) collective-permute-start(bf16[112,2048]{1,0:T(8,128)(2,1)S(1)} %fusion.21), channel_id=1, source_target_pairs={{0,128},{128,256},{256,384},{384,0},{1,129},{129,257},{257,385},{3... | collective-permute-start | bytes 1376264 | tf_op jit(solution)/shard_map/ppermute | solution.py:16
Sparse Core Ops, SparseCore 0:
  10.1 26.8 all-gather.6
  39.1 21.3 all-gather.8
  62.6 21.3 all-gather.10
  497.4 335.7 all-reduce.6
where the time goes:
time: 1100 us
  waiting for transfers between devices  549 us (50%)
  blocking collectives  372 us (34%)
  starting transfers between devices  69.6 us (6%)
  local copies, waits for them, and re-layouts  42.3 us (4%)
  other arithmetic  25.2 us (2%)
  matrix products  23.5 us (2%)
  between operations  14.8 us (1%)
    psum x1, waiting for transfers between devices, body(): router_sum, gain_sum = lax.psum((router_term, gain_term), ('expert', 'dp'))  279 us
    psum x1, blocking collectives, body(): router_sum, gain_sum = lax.psum((router_term, gain_term), ('expert', 'dp'))  252 us
    ppermute x3, waiting for transfers between devices, partner_2(): lax.ppermute(shard, axis, [(i, i ^ 1 << stride) for i in range(lax.axis_s...  85.8 us
    all_to_all x1, blocking collectives, body(): lax.all_to_all(send_grads, 'expert', split_axis=0, concat_axis=0, tiled=T...  60.5 us
    all_to_all x1, blocking collectives, body(): lax.all_to_all(send_rows, 'expert', split_axis=0, concat_axis=0, tiled=True)  60.2 us
    all_to_all x1, waiting for transfers between devices, body(): lax.all_to_all(expert_out, 'expert', split_axis=0, concat_axis=0, tiled=T...  49.7 us
    all_to_all x1, waiting for transfers between devices, body(): lax.all_to_all(grad_normed_rows, 'expert', split_axis=0, concat_axis=0, t...  48.8 us
    all_to_all x1, waiting for transfers between devices, body(): lax.all_to_all(output, 'expert', split_axis=0, concat_axis=0, tiled=True)  44.7 us
  transfers between devices with their start and end apart: 13, of which 9 were waited for; matrix products, arithmetic and copies ran while one was open for 3% of the time, Pallas kernels for 0%

commit v1 on v0

v1 whole, which is shorter than its diff:
```python
import jax
import jax.numpy as jnp
from jax import lax
from jax.experimental import pallas as pl
from jax.experimental.pallas import tpu as pltpu
from jax.sharding import PartitionSpec as P

EPS = 1e-06
MOST = 8
ROWS_Z = 16
PAIRS = 8
MESH = pl.DeviceIdType.MESH
F32 = jnp.float32
BF16 = jnp.bfloat16


class Place:
    def __init__(self):
        self.seg = lax.axis_index("segment")
        self.exp = lax.axis_index("expert")
        self.dp = lax.axis_index("dp")
        self.y = self.exp // ROWS_Z
        self.z = self.exp % ROWS_Z
        self.zp = self.z // 2
        self.par = self.z % 2
        self.ny = lax.axis_size("expert") // ROWS_Z

    def owner(self, j):
        rel = j % PAIRS
        y = (self.y + j // PAIRS) % self.ny
        zp = (self.zp + rel) % PAIRS
        turn = (rel - self.par + PAIRS) % PAIRS
        exp = y * ROWS_Z + zp * 2 + turn // 4
        return (self.seg, exp, self.dp), y * PAIRS + zp, self.y * PAIRS + self.par * 4 + turn % 4

    def client(self, j):
        r = (7 * self.par + j % PAIRS) % PAIRS
        y = (self.y + j // PAIRS) % self.ny
        par = r // 4
        zp = (self.zp + 2 * PAIRS - (4 * self.par + r % 4 + par)) % PAIRS
        return (self.seg, y * ROWS_Z + zp * 2 + par, self.dp), y * PAIRS + r

    def expert(self):
        return self.y * PAIRS + self.zp

    def core(self):
        return (self.seg, self.exp, 1 - self.dp)

    def twin(self):
        return (self.seg, self.exp + 1 - 2 * self.par, self.dp)


def signal(sem, device):
    pl.semaphore_signal(sem, inc=1, device_id=device, device_id_type=MESH)


def remote(src, dst, send, recv, device):
    return pltpu.make_async_remote_copy(
        src_ref=src, dst_ref=dst, send_sem=send, recv_sem=recv, device_id=device, device_id_type=MESH
    )


def out_kernel(
    send_a, send_b, send_g, wg, wu, wd, rows, grads, gate, up, down,
    send_sem, recv_sem, own_sem, wsend, wrecv, wown,
):
    me = Place()
    count = send_a.shape[0]
    barrier = pltpu.get_barrier_semaphore()

    @pl.loop(1, count)
    def _(j):
        signal(barrier, me.client(j)[0])

    signal(barrier, me.core())
    signal(barrier, me.twin())
    pl.semaphore_wait(barrier, count + 1)

    quarter = wg.shape[0]
    weights = ((wg, gate), (wu, up), (wd, down))

    def part(ref, k):
        return ref.at[pl.ds(k * quarter, quarter)]

    for m, (own, full) in enumerate(weights):
        remote(own, part(full, 2), wsend.at[0, m], wrecv.at[0, m], me.twin()).start()
        remote(own, part(full, 1), wsend.at[1, m], wrecv.at[1, m], me.core()).start()
        pltpu.make_async_copy(own, part(full, 0), wown.at[m]).start()
    streams = ((send_a, rows.at[0]), (send_b, rows.at[1]), (send_g, grads))

    for k, (src, dst) in enumerate(streams):
        _, expert, slot = me.owner(0)
        pltpu.make_async_copy(src.at[expert], dst.at[slot], own_sem.at[k]).start()

        @pl.loop(1, count)
        def _(j):
            device, expert, slot = me.owner(j)
            remote(src.at[expert], dst.at[slot], send_sem.at[k], recv_sem.at[k], device).start()

    for m, (own, full) in enumerate(weights):
        remote(own, part(full, 2), wsend.at[0, m], wrecv.at[0, m], me.twin()).wait_recv()
        remote(part(full, 2), part(full, 3), wsend.at[2, m], wrecv.at[2, m], me.core()).start()
    for k, (src, dst) in enumerate(streams):
        whole = remote(
            src.at[pl.ds(0, count - 1)], dst.at[pl.ds(0, count - 1)], send_sem.at[k], recv_sem.at[k], me.core()
        )
        whole.wait_recv()
        whole.wait_send()
        pltpu.make_async_copy(src.at[0], dst.at[0], own_sem.at[k]).wait()
    for m, (own, full) in enumerate(weights):
        remote(own, part(full, 2), wsend.at[0, m], wrecv.at[0, m], me.twin()).wait_send()
        remote(own, part(full, 1), wsend.at[1, m], wrecv.at[1, m], me.core()).wait()
        remote(part(full, 2), part(full, 3), wsend.at[2, m], wrecv.at[2, m], me.core()).wait()
        pltpu.make_async_copy(own, part(full, 0), wown.at[m]).wait()


def back_kernel(out_a, out_b, dots, back, dots_back, send_sem, recv_sem, own_sem):
    me = Place()
    count = out_a.shape[0]
    barrier = pltpu.get_barrier_semaphore()

    @pl.loop(1, count)
    def _(j):
        signal(barrier, me.owner(j)[0])

    pl.semaphore_wait(barrier, count - 1)
    streams = ((dots, dots_back), (out_a, back.at[0]), (out_b, back.at[1]))
    expert = me.expert()
    for k, (src, dst) in enumerate(streams):
        _, slot = me.client(0)
        pltpu.make_async_copy(src.at[slot], dst.at[expert], own_sem.at[k]).start()

        @pl.loop(1, count)
        def _(j):
            device, slot = me.client(j)
            remote(src.at[slot], dst.at[expert], send_sem.at[k], recv_sem.at[k], device).start()

    for k, (src, dst) in enumerate(streams):
        whole = remote(
            src.at[pl.ds(0, count - 1)], dst.at[pl.ds(0, count - 1)], send_sem.at[k], recv_sem.at[k], me.core()
        )
        whole.wait_recv()
        whole.wait_send()
        pltpu.make_async_copy(src.at[0], dst.at[0], own_sem.at[k]).wait()


def sum_kernel(
    part, act, grad, total, next_act, prev_grad, held, got, line,
    shift_send, shift_recv, ssem, rsem,
):
    me = Place()
    ny = me.ny
    group = 2 * ny
    mine = me.y * 2 + me.dp
    barrier = pltpu.get_barrier_semaphore()
    after = ((me.seg + 1) % 4, me.exp, me.dp)
    before = ((me.seg + 3) % 4, me.exp, me.dp)

    def in_row(o):
        other = (mine + o) % group
        return other, (me.seg, (other // 2) * ROWS_Z + me.z, other % 2)

    def in_column(o):
        other = (me.z + o) % ROWS_Z
        return other, (me.seg, me.y * ROWS_Z + other, me.dp)

    signal(barrier, after)
    signal(barrier, before)

    @pl.loop(1, group)
    def _(o):
        signal(barrier, in_row(o)[1])

    @pl.loop(1, ROWS_Z)
    def _(o):
        signal(barrier, in_column(o)[1])

    pl.semaphore_wait(barrier, 2 + group - 1 + ROWS_Z - 1)
    go_next = remote(act, next_act, shift_send.at[0], shift_recv.at[0], after)
    go_prev = remote(grad, prev_grad, shift_send.at[1], shift_recv.at[1], before)

    @pl.loop(1, group)
    def _(o):
        other, device = in_row(o)
        remote(part.at[other], got.at[o - 1], ssem.at[0], rsem.at[0], device).start()

    go_next.start()
    go_prev.start()
    whole = remote(part.at[pl.ds(0, group - 1)], got, ssem.at[0], rsem.at[0], after)
    whole.wait_recv()
    held[...] = part[mine] + jnp.sum(got[...], 0)

    @pl.loop(1, ROWS_Z)
    def _(o):
        other, device = in_column(o)
        remote(held.at[other], line.at[o - 1], ssem.at[1], rsem.at[1], device).start()

    second = remote(held.at[pl.ds(0, ROWS_Z - 1)], line, ssem.at[1], rsem.at[1], after)
    second.wait_recv()
    total[mine, me.z] = held[me.z] + jnp.sum(line[...], 0)

    @pl.loop(1, ROWS_Z)
    def _(o):
        _, device = in_column(o)
        here = total.at[mine, me.z]
        remote(here, here, ssem.at[2], rsem.at[2], device).start()

    third = remote(
        total.at[mine, pl.ds(0, ROWS_Z - 1)], total.at[mine, pl.ds(0, ROWS_Z - 1)], ssem.at[2], rsem.at[2], after
    )
    third.wait_recv()

    @pl.loop(1, group)
    def _(o):
        _, device = in_row(o)
        remote(total.at[mine], total.at[mine], ssem.at[3], rsem.at[3], device).start()

    fourth = remote(
        total.at[pl.ds(0, group - 1)], total.at[pl.ds(0, group - 1)], ssem.at[3], rsem.at[3], after
    )
    fourth.wait_recv()
    whole.wait_send()
    second.wait_send()
    third.wait_send()
    fourth.wait_send()
    go_next.wait()
    go_prev.wait()


ANY = pl.BlockSpec(memory_space=pl.ANY)
VMEM = pl.BlockSpec(memory_space=pltpu.VMEM)


def params(number):
    return pltpu.CompilerParams(collective_id=number, has_side_effects=True, vmem_limit_bytes=32 << 20)


def like(shape, dtype):
    return jax.ShapeDtypeStruct(shape, dtype)


def prepare(x_block, route, gain, router_w):
    tokens = x_block.shape[0]
    experts = router_w.shape[0]
    x_float = x_block.astype(F32)
    inv_rms = lax.rsqrt(jnp.mean(x_float * x_float, -1, keepdims=True) + EPS)
    normed = (x_float * inv_rms * gain[None, :]).astype(BF16)
    logits = jnp.einsum("td,ed->te", normed, router_w, preferred_element_type=F32)
    ids = jnp.arange(experts, dtype=jnp.int32)[None, :]
    hot = (route[:, 0:1] == ids, route[:, 1:2] == ids)
    chosen = [jnp.sum(jnp.where(h, logits, 0.0), -1, keepdims=True) for h in hot]
    weights = (jax.nn.sigmoid(chosen[0] - chosen[1]), jax.nn.sigmoid(chosen[1] - chosen[0]))
    below = jnp.arange(tokens)[:, None] > jnp.arange(tokens)[None, :]
    counts = jnp.dot(below.astype(BF16), (hot[0] | hot[1]).astype(BF16), preferred_element_type=F32)
    slots = jnp.arange(experts * MOST, dtype=jnp.int32)[None, :]
    picks = []
    for k in range(2):
        rank = jnp.sum(jnp.where(hot[k], counts, 0.0), -1, keepdims=True).astype(jnp.int32)
        picks.append(route[:, k : k + 1] * MOST + rank == slots)
    return x_float, inv_rms, normed, hot, weights, picks


def to_slots(picks, rows):
    both = (picks[0] | picks[1]).astype(BF16)
    out = lax.dot_general(both, rows, (((0,), (0,)), ((), ())), preferred_element_type=F32)
    return out.astype(BF16).reshape(-1, MOST, rows.shape[1])


def from_slots(pick, slots):
    return jnp.dot(pick.astype(BF16), slots, preferred_element_type=F32)


def dot_t(a, b):
    return lax.dot_general(a, b, (((1,), (1,)), ((), ())), preferred_element_type=F32)


def body(
    act_in, stash_in, grad_in, route_a, route_b, norm_gain, router, gate_weight, up_weight, down_weight
):
    gain = norm_gain[0]
    router_w = router[0]
    experts, width = router_w.shape
    blocks = lax.axis_size("expert") * lax.axis_size("dp")
    grad = grad_in[0]
    x_a, _, normed_a, _, weights_a, picks_a = prepare(act_in[0], route_a[0], gain, router_w)
    x_b, inv_b, normed_b, hot_b, weights_b, picks_b = prepare(stash_in[0], route_b[0], gain, router_w)
    send_a = to_slots(picks_a, normed_a)
    send_b = to_slots(picks_b, normed_b)
    send_g = to_slots(picks_b, grad)
    quarters = (gate_weight[0, 0], up_weight[0, 0], down_weight[0, 0])
    quarter = quarters[0].shape[0]
    block = (experts, MOST, width)
    dma = pltpu.SemaphoreType.DMA
    rows, grads, gate, up, down = pl.pallas_call(
        out_kernel,
        out_shape=[like((2, *block), BF16), like(block, BF16)] + [like((4 * quarter, width), BF16)] * 3,
        in_specs=[ANY] * 6,
        out_specs=[ANY] * 5,
        scratch_shapes=[dma((3,)), dma((3,)), dma((3,)), dma((3, 3)), dma((3, 3)), dma((3,))],
        compiler_params=params(0),
    )(send_a, send_b, send_g, *quarters)

    slots = experts * MOST
    rows = rows.reshape(2 * slots, width)
    gate_val = dot_t(rows, gate)
    up_val = dot_t(rows, up)
    hidden = (jax.nn.silu(gate_val) * up_val).astype(BF16)
    out_a = jnp.dot(hidden[:slots], down, preferred_element_type=F32).astype(BF16).reshape(block)
    grad_hidden = dot_t(grads.reshape(slots, width), down)
    dots = jnp.sum(hidden[slots:].astype(F32) * grad_hidden, -1)
    dots = jnp.pad(dots.reshape(experts, 1, MOST), ((0, 0), (0, 0), (0, 128 - MOST)))
    gate_b, up_b = gate_val[slots:], up_val[slots:]
    sigma = jax.nn.sigmoid(gate_b)
    grad_gate = (grad_hidden * up_b * sigma * (1.0 + gate_b * (1.0 - sigma))).astype(BF16)
    grad_up = (grad_hidden * gate_b * sigma).astype(BF16)
    out_b = jnp.dot(grad_gate, gate, preferred_element_type=F32)
    out_b = out_b + jnp.dot(grad_up, up, preferred_element_type=F32)
    out_b = out_b.astype(BF16).reshape(block)

    back, dots_back = pl.pallas_call(
        back_kernel,
        out_shape=[like((2, *block), BF16), like((experts, 1, 128), F32)],
        in_specs=[ANY] * 3,
        out_specs=[ANY] * 2,
        scratch_shapes=[dma((3,)), dma((3,)), dma((3,))],
        compiler_params=params(1),
    )(out_a, out_b, dots)

    back = back.reshape(2, slots, width)
    mixed = x_a + weights_a[0] * from_slots(picks_a[0], back[0]) + weights_a[1] * from_slots(picks_a[1], back[0])
    dots_back = dots_back[:, 0, :MOST].reshape(1, slots)
    dot_of = [jnp.sum(jnp.where(pick, dots_back, 0.0), -1, keepdims=True) for pick in picks_b]
    logit_grad = weights_b[0] * weights_b[1] * (dot_of[0] - dot_of[1])
    dlogits = (logit_grad * (hot_b[0].astype(F32) - hot_b[1].astype(F32))).astype(BF16)
    out_grad = grad.astype(F32)
    dnormed = (
        weights_b[0] * from_slots(picks_b[0], back[1])
        + weights_b[1] * from_slots(picks_b[1], back[1])
        + jnp.dot(dlogits, router_w, preferred_element_type=F32)
    )
    router_term = lax.dot_general(dlogits, normed_b, (((0,), (0,)), ((), ())), preferred_element_type=F32)
    gain_term = jnp.sum(dnormed * x_b * inv_b, 0)
    dxn = dnormed * gain[None, :]
    input_grad = out_grad + inv_b * dxn - x_b * inv_b**3 * jnp.mean(dxn * x_b, -1, keepdims=True)
    group = blocks // ROWS_Z
    wide = width // ROWS_Z
    term = jnp.concatenate(
        [
            router_term.reshape(group, experts // group, ROWS_Z, wide).transpose(0, 2, 1, 3),
            jnp.pad(gain_term.reshape(1, ROWS_Z, 1, wide), ((0, group - 1), (0, 0), (0, 0), (0, 0))),
            jnp.zeros((group, ROWS_Z, 8 - experts // group - 1, wide), F32),
        ],
        2,
    )
    total, next_act, prev_grad = pl.pallas_call(
        sum_kernel,
        out_shape=[like(term.shape, F32), like(grad.shape, BF16), like(grad.shape, BF16)],
        in_specs=[VMEM, ANY, ANY],
        out_specs=[VMEM, ANY, ANY],
        scratch_shapes=[
            pltpu.VMEM(term.shape[1:], F32),
            pltpu.VMEM((group - 1, *term.shape[1:]), F32),
            pltpu.VMEM((ROWS_Z - 1, *term.shape[2:]), F32),
            dma((2,)), dma((2,)), dma((4,)), dma((4,)),
        ],
        compiler_params=params(2),
    )(term, mixed.astype(BF16), input_grad.astype(BF16))
    total = total / blocks
    router_grad = total[:, :, : experts // group].transpose(0, 2, 1, 3).reshape(experts, width)
    gain_grad = total[0, :, experts // group].reshape(width)
    return next_act[None], prev_grad[None], router_grad[None], gain_grad[None]


def solution(mesh):
    tokens = P("segment", ("expert", "dp"), None)
    weight = P("segment", "expert", "dp", None)
    router = P("segment", None, None)
    gain = P("segment", None)
    return jax.shard_map(
        body,
        mesh=mesh,
        in_specs=(tokens, tokens, tokens, tokens, tokens, gain, router, weight, weight, weight),
        out_specs=(tokens, tokens, router, gain),
        check_vma=False,
    )
```

time: 1100 us -> 333 us (0.30)
  waiting for transfers between devices: 549 us -> 0 us
  blocking collectives: 372 us -> 0 us
  Pallas kernels: 0 us -> 307 us
  starting transfers between devices: 69.6 us -> 0 us
  local copies, waits for them, and re-layouts: 42.3 us -> 4.44 us
  other arithmetic: 25.2 us -> 3.08 us
  between operations: 14.8 us -> 1.02 us
    pallas_call x0 -> x3, Pallas kernels: none -> 307 us  [the longest x1 165 us: body(): pl.pallas_call(out_kernel, out_shape=[like((2, *block), BF16), like(block...]
    psum x1 -> x0, waiting for transfers between devices: 279 us -> none  [body(): router_sum, gain_sum = lax.psum((router_term, gain_term), ('expert', 'dp'))]
    psum x1 -> x0, blocking collectives: 252 us -> none  [body(): router_sum, gain_sum = lax.psum((router_term, gain_term), ('expert', 'dp'))]
    all_to_all x4 -> x0, waiting for transfers between devices: 143 us -> none  [the longest x1 49.7 us: body(): lax.all_to_all(expert_out, 'expert', split_axis=0, concat_axis=0, tiled=T...]
    all_to_all x2 -> x0, blocking collectives: 121 us -> none  [the longest x1 60.5 us: body(): lax.all_to_all(send_grads, 'expert', split_axis=0, concat_axis=0, tiled=T...]
    ppermute x5 -> x0, waiting for transfers between devices: 85.8 us -> none  [the longest x3 85.8 us: partner_2(): lax.ppermute(shard, axis, [(i, i ^ 1 << stride) for i in range(lax.axis_s...]
    all_to_all x4 -> x0, starting transfers between devices: 54.7 us -> none  [the longest x1 19.3 us: body(): lax.all_to_all(send_rows, 'expert', split_axis=0, concat_axis=0, tiled=True)]
    all_gather x3 -> x0, waiting for transfers between devices: 38.7 us -> none  [the longest x1 21.4 us: body(): lax.all_gather(quarters[2], 'dp', axis=0, tiled=True)]
  transfers between devices with their start and end apart: 13 -> 0, of which waited for: 9 -> 0; matrix products, arithmetic and copies ran while one was open for 3% -> 0% of each run, Pallas kernels for 0% -> 0%
where the time goes in v1:
time: 333 us; the launch traced here: 332 us
  Pallas kernels  307 us (92%)
  matrix products  16.5 us (5%)
  local copies, waits for them, and re-layouts  4.44 us (1%)
    pallas_call x1, Pallas kernels, body(): pl.pallas_call(out_kernel, out_shape=[like((2, *block), BF16), like(block...  165 us
    pallas_call x1, Pallas kernels, body(): pl.pallas_call(back_kernel, out_shape=[like((2, *block), BF16), like((exp...  98.1 us
    pallas_call x1, Pallas kernels, body(): pl.pallas_call(sum_kernel, out_shape=[like(term.shape, F32), like(grad.sh...  44.4 us

profile of v1, /device:TPU:1, one launch (start us, length us, event | category | flops | bytes accessed | tf_op | source)
XLA Modules:
  0.0 332.3 jit_solution(342488409673419982)
XLA Ops:
  0.6 0.0 copy-start
  0.6 0.0 copy-start.8
  0.7 1.3 fusion.27
  1.9 0.0 copy-start.6
  2.0 0.0 copy-start.10
  2.0 1.4 fusion.53
  3.4 0.8 slice_bitcast_fusion.5
  4.2 0.2 select_reduce_fusion.7
  4.3 0.8 fusion.110
  5.1 1.6 fusion.3.send_b
  6.7 0.0 copy-start.1
  6.7 0.0 copy-start.2
  6.7 0.0 copy-start.3
  6.7 0.6 fusion.4.send_g
  7.3 0.2 fusion.38
  7.5 0.3 fusion.49
  7.8 0.2 select_reduce_fusion.6
  8.0 0.5 fusion.2.send_a
  8.6 164.8 %shard_map.129 = (bf16[2,32,8,2048]{3,2,1,0:T(8,128)(2,1)S(1)}, bf16[32,8,2048]{2,1,0:T(8,128)(2,1)S(1)}, bf16[704,2048]{1,0:T(8,128)(2,1)S(1)}, bf16[704,2048]{1,0:T(8,128)(2,1)S(1)}, bf16[704,2048]{1,0:T(8,128)(2,1)S(1)}) custom-call(bf16[32,8,2048]{2,1,0:T(8,128)(2,1)S(1)} %fusion.2.send_a, bf16[32,8,2048]{2,1,0:T(8,128)(2,1)S(1)} %fusion.3.send_b, ...), custom_call_target="tpu_custom_call" | custom-call | tf_op jit(solution)/shard_map/pallas_call | solution.py:294
  173.4 1.7 fusion.113
  175.1 1.8 multiply_convert_fusion
  177.0 1.0 multiply_reduce_fusion
  178.0 1.1 fusion.63
  179.1 1.0 fusion.5.out_b
  180.1 0.1 reshape.251
  180.2 2.9 fusion.1.out_a
  183.2 0.0 copy-start.7
  183.2 98.1 %shard_map.130 = (bf16[2,32,8,2048]{3,2,1,0:T(8,128)(2,1)S(1)}, f32[32,1,128]{2,1,0:T(1,128)S(1)}) custom-call(bf16[32,8,2048]{2,1,0:T(8,128)(2,1)S(1)} %fusion.1.out_a, bf16[32,8,2048]{2,1,0:T(8,128)(2,1)S(1)} %fusion.5.out_b, f32[32,1,128]{2,1,0:T(1,128)S(1)} %pad.8.dots), custom_call_target="tpu_custom_call" | custom-call | tf_op jit(solution)/shard_map/pallas_call | solution.py:320
  281.4 0.0 copy-done.7
  281.4 0.3 fusion.7
  281.7 0.3 fusion.9.act
  282.1 0.1 broadcast_in_dim.60
  282.2 0.2 select_reduce_fusion
  282.4 0.0 copy-start.5
  282.4 0.3 convolution_multiply_fusion.3
  282.8 0.0 copy-start.9
  282.8 0.3 fusion.8
  283.2 0.3 copy-done.5
  283.5 0.5 fusion.35
  284.0 0.5 fusion.34
  284.5 0.3 convolution_bitcast_fusion
  284.8 0.1 pad.12.clone
  284.9 0.1 fusion.46.part
  285.0 44.4 %shard_map.131 = (f32[8,16,8,128]{3,2,1,0:T(8,128)S(1)}, bf16[112,2048]{1,0:T(8,128)(2,1)S(1)}, bf16[112,2048]{1,0:T(8,128)(2,1)S(1)}) custom-call(f32[8,16,8,128]{3,2,1,0:T(8,128)S(1)} %fusion.46.part, bf16[112,2048]{1,0:T(8,128)(2,1)S(1)} %fusion.9.act, bf16[112,2048]{1,0:T(8,128)(2,1)S(1)} %get-tuple-element.43.grad), custom_call_target="tpu_custom_call" | custom-call | tf_op jit(solution)/shard_map/pallas_call | solution.py:355
  329.5 0.7 broadcast_in_dim_reshape.3
  330.2 0.6 slice_bitcast_fusion.1
  330.8 0.8 copy.31
  331.6 0.8 copy.32
  (28 shorter events, 0.3 us)
Async XLA Ops:
  0.6 1.3 copy-start
  0.6 6.0 %copy-start.8 = (bf16[1,112,2048]{2,1,0:T(8,128)(2,1)S(1)}, bf16[1,112,2048]{2,1,0:T(8,128)(2,1)}, u32[]{:S(2)}) copy-start(bf16[1,112,2048]{2,1,0:T(8,128)(2,1)} %param.12) | copy-start | bytes 1376260
  1.9 5.3 %copy-start.6 = (bf16[1,112,2048]{2,1,0:T(8,128)(2,1)S(1)}, bf16[1,112,2048]{2,1,0:T(8,128)(2,1)}, u32[]{:S(2)}) copy-start(bf16[1,112,2048]{2,1,0:T(8,128)(2,1)} %param.10) | copy-start | bytes 1376260
  2.0 5.5 %copy-start.10 = (f32[1,2048]{1,0:T(1,128)S(1)}, f32[1,2048]{1,0:T(1,128)}, u32[]{:S(2)}) copy-start(f32[1,2048]{1,0:T(1,128)} %param.15) | copy-start | bytes 24580
  5.1 2.7 copy-start.11
  6.7 1.9 copy-start.1
  6.7 1.9 copy-start.2
  6.7 1.9 copy-start.3
  173.4 3.6 %copy-start.4 = (bf16[704,2048]{1,0:T(8,128)(2,1)}, bf16[704,2048]{1,0:T(8,128)(2,1)S(1)}, u32[]{:S(2)}) copy-start(bf16[704,2048]{1,0:T(8,128)(2,1)S(1)} %get-tuple-element.17) | copy-start | bytes 8650756
  177.0 1.0 copy-start.12
  183.2 98.2 %copy-start.7 = (bf16[1,112,2048]{2,1,0:T(8,128)(2,1)S(1)}, bf16[1,112,2048]{2,1,0:T(8,128)(2,1)}, u32[]{:S(2)}) copy-start(bf16[1,112,2048]{2,1,0:T(8,128)(2,1)} %param.10) | copy-start | bytes 1376260
  282.4 1.0 copy-start.5
  282.8 1.2 copy-start.9

commit v2 on v1

v2 whole, which is shorter than its diff:
```python
import jax
import jax.numpy as jnp
from jax import lax
from jax.experimental import pallas as pl
from jax.experimental.pallas import tpu as pltpu
from jax.sharding import PartitionSpec as P

EPS = 1e-06
MOST = 8
ROWS_Z = 16
PAIRS = 8
MESH = pl.DeviceIdType.MESH
F32 = jnp.float32
BF16 = jnp.bfloat16


class Place:
    def __init__(self):
        self.seg = lax.axis_index("segment")
        self.exp = lax.axis_index("expert")
        self.dp = lax.axis_index("dp")
        self.y = self.exp // ROWS_Z
        self.z = self.exp % ROWS_Z
        self.zp = self.z // 2
        self.par = self.z % 2
        self.ny = lax.axis_size("expert") // ROWS_Z

    def owner(self, j):
        rel = j % PAIRS
        y = (self.y + j // PAIRS) % self.ny
        zp = (self.zp + rel) % PAIRS
        turn = (rel - self.par + PAIRS) % PAIRS
        exp = y * ROWS_Z + zp * 2 + turn // 4
        return (self.seg, exp, self.dp), y * PAIRS + zp, self.y * PAIRS + self.par * 4 + turn % 4

    def client(self, j):
        r = (7 * self.par + j % PAIRS) % PAIRS
        y = (self.y + j // PAIRS) % self.ny
        par = r // 4
        zp = (self.zp + 2 * PAIRS - (4 * self.par + r % 4 + par)) % PAIRS
        return (self.seg, y * ROWS_Z + zp * 2 + par, self.dp), y * PAIRS + r

    def expert(self):
        return self.y * PAIRS + self.zp

    def core(self):
        return (self.seg, self.exp, 1 - self.dp)

    def twin(self):
        return (self.seg, self.exp + 1 - 2 * self.par, self.dp)


def signal(sem, device):
    pl.semaphore_signal(sem, inc=1, device_id=device, device_id_type=MESH)


def remote(src, dst, send, recv, device):
    return pltpu.make_async_remote_copy(
        src_ref=src, dst_ref=dst, send_sem=send, recv_sem=recv, device_id=device, device_id_type=MESH
    )


def dot(a, b, dims=((1,), (0,))):
    return lax.dot_general(a, b, (dims, ((), ())), preferred_element_type=F32)


def dot_t(a, b):
    return dot(a, b, ((1,), (1,)))


def iota(shape, axis):
    return lax.broadcasted_iota(jnp.int32, shape, axis)


def ones(mask):
    return jnp.where(mask, 1.0, 0.0)


def norm_of(x):
    x_float = x.astype(F32)
    inv_rms = lax.rsqrt(jnp.mean(x_float * x_float, -1, keepdims=True) + EPS)
    return x_float, inv_rms


def prepare(x, route, gain, router_w):
    tokens = x.shape[0]
    experts = router_w.shape[0]
    x_float, inv_rms = norm_of(x)
    normed = (x_float * inv_rms * gain).astype(BF16)
    logits = dot_t(normed, router_w)
    ids = iota((tokens, experts), 1)
    hot = [ones(route[:, k : k + 1] == ids) for k in range(2)]
    chosen = [jnp.sum(h * logits, -1, keepdims=True) for h in hot]
    weights = (jax.nn.sigmoid(chosen[0] - chosen[1]), jax.nn.sigmoid(chosen[1] - chosen[0]))
    below = ones(iota((tokens, tokens), 0) > iota((tokens, tokens), 1)).astype(BF16)
    counts = dot(below, (hot[0] + hot[1]).astype(BF16))
    slots = iota((tokens, experts * MOST), 1)
    picks = []
    for k in range(2):
        rank = jnp.sum(hot[k] * counts, -1, keepdims=True).astype(jnp.int32)
        picks.append(ones(route[:, k : k + 1] * MOST + rank == slots))
    return normed, weights, picks


def to_slots(both, rows):
    out = dot(both, rows, ((0,), (0,)))
    return out.reshape(out.shape[0] // MOST, MOST, out.shape[1]).astype(BF16)


def flat(blocks):
    return blocks.astype(F32).reshape(blocks.shape[0] * MOST, blocks.shape[2]).astype(BF16)


def kernel(
    act, stash, grad, route_a, route_b, gain, router, wg, wu, wd,
    next_act, prev_grad, router_out, gain_out,
    send_a, send_b, send_g, rec_a, rec_b, rec_g, rows, grads, gate, up, down, acc,
    out_a, out_b, back_a, back_b, normed_b, mixed,
    stash_s, grad_s, picks_b, picks_s, router_s, gain_s, dlog, dlog_s,
    p_send, p_rec, q_send, q_back, rsum, term, held, got, line, total,
    ssem, rsem, own, shift_send, shift_recv, wsend, wrecv, wown, sum_send, sum_recv,
):
    me = Place()
    count = send_a.shape[0]
    tokens = act.shape[0]
    quarters = gate.shape[0]
    width = act.shape[1]
    group = 2 * me.ny
    mine = me.y * 2 + me.dp
    behind, ahead = (me.seg + 3) % 4, (me.seg + 1) % 4
    before = (behind, me.exp, me.dp)
    after = (ahead, me.exp, me.dp)
    barrier = pltpu.get_barrier_semaphore()

    def in_row(o):
        other = (mine + o) % group
        return other, (me.seg, (other // 2) * ROWS_Z + me.z, other % 2)

    def in_column(o):
        other = (me.z + o) % ROWS_Z
        return other, (me.seg, me.y * ROWS_Z + other, me.dp)

    signal(barrier, before)
    signal(barrier, me.core())
    signal(barrier, me.twin())
    signal(barrier, after)

    @pl.loop(1, count)
    def _(j):
        signal(barrier, me.client(j)[0])
        device = me.owner(j)[0]
        signal(barrier, device)
        signal(barrier, (ahead, device[1], device[2]))

    @pl.loop(1, group)
    def _(o):
        signal(barrier, in_row(o)[1])

    @pl.loop(1, ROWS_Z)
    def _(o):
        signal(barrier, in_column(o)[1])

    pl.semaphore_wait(barrier, 4 + 3 * (count - 1) + group - 1 + ROWS_Z - 1)

    weights = ((wg, gate), (wu, up), (wd, down))

    def to_twin(m):
        return remote(weights[m][0], weights[m][1].at[2], wsend.at[0, m], wrecv.at[0, m], me.twin())

    def to_core(m):
        return remote(weights[m][0], weights[m][1].at[1], wsend.at[1, m], wrecv.at[1, m], me.core())

    def on_to_core(m):
        full = weights[m][1]
        return remote(full.at[2], full.at[3], wsend.at[2, m], wrecv.at[2, m], me.core())

    def to_self(m):
        return pltpu.make_async_copy(weights[m][0], weights[m][1].at[0], wown.at[m])

    def shift(k, src, dst, device):
        return remote(src, dst, shift_send.at[k], shift_recv.at[k], device)

    shifts = [
        shift(0, stash, stash_s, before),
        shift(1, grad, grad_s, before),
        shift(2, router, router_s, before),
        shift(3, gain, gain_s, before),
        shift(4, picks_b, picks_s, before),
        shift(5, dlog, dlog_s, before),
        shift(6, mixed, next_act, after),
    ]

    def send(k, src, dst, block=lambda e: e):
        _, expert, slot = me.owner(0)
        pltpu.make_async_copy(src.at[block(expert)], dst.at[slot], own.at[k]).start()

        @pl.loop(1, count)
        def _(j):
            device, expert, slot = me.owner(j)
            remote(src.at[block(expert)], dst.at[slot], ssem.at[k], rsem.at[k], device).start()

    def send_back(k, src, dst):
        expert = me.expert()
        pltpu.make_async_copy(src.at[me.client(0)[1]], dst.at[expert], own.at[k]).start()

        @pl.loop(1, count)
        def _(j):
            device, slot = me.client(j)
            remote(src.at[slot], dst.at[expert], ssem.at[k], rsem.at[k], device).start()

    def others(k, ref):
        part = ref.at[pl.ds(0, count - 1)]
        return remote(part, part, ssem.at[k], rsem.at[k], after)

    def arrived(k, ref):
        others(k, ref).wait_recv()
        pltpu.make_async_copy(ref.at[0], ref.at[0], own.at[k]).wait()

    for m in range(3):
        to_twin(m).start()
        to_core(m).start()
        to_self(m).start()
    gain_row = gain[...]
    normed_a, weights_a, picks_a = prepare(act[...], route_a[...], gain_row, router[...])
    send_a[...] = to_slots((picks_a[0] + picks_a[1]).astype(BF16), normed_a)
    send(0, send_a, rec_a)
    for k in range(4):
        shifts[k].start()

    normed, weights_b, picks = prepare(stash[...], route_b[...], gain_row, router[...])
    normed_b[...] = normed
    both = (picks[0] + picks[1]).astype(BF16)
    picks_b[...] = both
    shifts[4].start()
    send_b[...] = to_slots(both, normed)
    send(1, send_b, rec_b)
    send_g[...] = to_slots(both, grad[...])
    send(2, send_g, rec_g)
    p_row = jnp.sum(picks[0] * weights_b[0] + picks[1] * weights_b[1], 0, keepdims=True)
    halves = p_send.shape[0]
    for h in range(halves):
        p_send[h] = p_row[:, h * 128 : (h + 1) * 128]
    per_half = count // halves
    send(3, p_send, p_rec, lambda e: e // per_half)

    for m in range(3):
        to_twin(m).wait_recv()
        on_to_core(m).start()
    arrived(0, rec_a)
    rows[...] = flat(rec_a[...])
    for m in range(3):
        to_core(m).wait_recv()
        on_to_core(m).wait_recv()
        to_self(m).wait()
    acc[...] = jnp.zeros_like(acc)

    @pl.loop(0, quarters)
    def _(c):
        gate_val = dot_t(rows[...], gate[c])
        up_val = dot_t(rows[...], up[c])
        hidden = (gate_val * jax.nn.sigmoid(gate_val) * up_val).astype(BF16)
        acc[...] += dot(hidden, down[c])

    out_a[...] = acc[...].reshape(out_a.shape).astype(BF16)
    arrived(1, rec_b)
    arrived(2, rec_g)
    arrived(3, p_rec)
    send_back(4, out_a, back_a)

    rows[...] = flat(rec_b[...])
    grads[...] = flat(rec_g[...])
    acc[...] = jnp.zeros_like(acc)
    slots = count * MOST

    def back_part(c, dots):
        gate_val = dot_t(rows[...], gate[c])
        up_val = dot_t(rows[...], up[c])
        grad_hidden = dot_t(grads[...], down[c])
        sigma = jax.nn.sigmoid(gate_val)
        silu = gate_val * sigma
        hidden = (silu * up_val).astype(BF16)
        grad_gate = (grad_hidden * up_val * sigma * (1.0 + gate_val * (1.0 - sigma))).astype(BF16)
        grad_up = (grad_hidden * silu).astype(BF16)
        acc[...] += dot(grad_gate, gate[c]) + dot(grad_up, up[c])
        return dots + jnp.sum(hidden.astype(F32) * grad_hidden, -1, keepdims=True)

    dots = lax.fori_loop(0, quarters, back_part, jnp.zeros((slots, 1), F32))
    base = (me.expert() % per_half) * MOST
    lanes = ones(iota((count, MOST, 128), 2) == iota((count, MOST, 128), 1) + base)
    q_send[...] = jnp.sum(lanes * dots.reshape(count, MOST, 1), 1, keepdims=True)
    send_back(5, q_send, q_back)
    p_col = jnp.sum(lanes * p_rec[...], 2, keepdims=True).reshape(slots, 1)
    scaled = acc[...] * p_col
    out_b[...] = scaled.reshape(out_b.shape).astype(BF16)
    expert = me.expert()

    @pl.loop(0, count)
    def _(j):
        device, slot = me.client(j)
        device = (behind, device[1], device[2])
        remote(out_b.at[slot], back_b.at[expert], ssem.at[6], rsem.at[6], device).start()

    gain_own = jnp.sum(scaled * rows[...].astype(F32), 0, keepdims=True) / gain_row

    arrived(5, q_back)
    q_all = q_back[...]
    q_row = jnp.concatenate(
        [jnp.sum(q_all[h * per_half : (h + 1) * per_half], 0) for h in range(halves)], 1
    )
    dot_of = [jnp.sum(pick * q_row, -1, keepdims=True) for pick in picks]
    logit_grad = weights_b[0] * weights_b[1] * (dot_of[0] - dot_of[1])
    ids = iota((tokens, 128), 1)
    route = route_b[...]
    signs = ones(route[:, 0:1] == ids) - ones(route[:, 1:2] == ids)
    dlogits = (logit_grad * signs).astype(BF16)
    dlog[...] = dlogits
    shifts[5].start()
    x_float, inv_rms = norm_of(stash[...])
    dlogits = dlogits[:, :count]
    rsum[...] = dot(dlogits, normed_b[...], ((0,), (0,)))
    gain_part = gain_own + jnp.sum(dot(dlogits, router[...]) * x_float * inv_rms, 0, keepdims=True)
    per = count // group
    term[...] = jnp.zeros_like(term)
    for g in range(group):
        for c in range(ROWS_Z):
            term[g, c, 0:per, :] = rsum[g * per : (g + 1) * per, c * 128 : (c + 1) * 128]
    for c in range(ROWS_Z):
        term[0, c, per : per + 1, :] = gain_part[:, c * 128 : (c + 1) * 128]

    @pl.loop(1, group)
    def _(o):
        other, device = in_row(o)
        remote(term.at[other], got.at[o - 1], sum_send.at[0], sum_recv.at[0], device).start()

    def summed(k, ref):
        return remote(ref, ref, sum_send.at[k], sum_recv.at[k], after)

    summed(0, got).wait_recv()
    held[...] = term[mine] + jnp.sum(got[...], 0)

    @pl.loop(1, ROWS_Z)
    def _(o):
        other, device = in_column(o)
        remote(held.at[other], line.at[o - 1], sum_send.at[1], sum_recv.at[1], device).start()

    summed(1, line).wait_recv()
    total[mine, me.z] = held[me.z] + jnp.sum(line[...], 0)

    @pl.loop(1, ROWS_Z)
    def _(o):
        here = total.at[mine, me.z]
        remote(here, here, sum_send.at[2], sum_recv.at[2], in_column(o)[1]).start()

    summed(2, line).wait_recv()

    @pl.loop(1, group)
    def _(o):
        remote(total.at[mine], total.at[mine], sum_send.at[3], sum_recv.at[3], in_row(o)[1]).start()

    arrived(4, back_a)
    returned = flat(back_a[...])
    mixed[...] = (
        act[...].astype(F32)
        + weights_a[0] * dot(picks_a[0].astype(BF16), returned)
        + weights_a[1] * dot(picks_a[1].astype(BF16), returned)
    ).astype(BF16)
    shifts[6].start()

    summed(3, got).wait_recv()
    scale = 1.0 / (group * ROWS_Z)
    for g in range(group):
        for c in range(ROWS_Z):
            router_out[g * per : (g + 1) * per, c * 128 : (c + 1) * 128] = total[g, c, 0:per, :] * scale
    for c in range(ROWS_Z):
        gain_out[:, c * 128 : (c + 1) * 128] = total[0, c, per : per + 1, :] * scale

    for k in range(6):
        shifts[k].wait_recv()
    x_float, inv_rms = norm_of(stash_s[...])
    acc[0:tokens, :] = dot(dlog_s[...][:, :count], router_s[...])
    remote(out_b, back_b, ssem.at[6], rsem.at[6], after).wait_recv()
    dnormed = acc[0:tokens, :] + dot(picks_s[...], flat(back_b[...]))
    dxn = dnormed * gain_s[...]
    prev_grad[...] = (
        grad_s[...].astype(F32)
        + inv_rms * dxn
        - x_float * (inv_rms * inv_rms * inv_rms * jnp.mean(dxn * x_float, -1, keepdims=True))
    ).astype(BF16)

    for m in range(3):
        to_twin(m).wait_send()
        to_core(m).wait_send()
        on_to_core(m).wait_send()
    for k, ref in enumerate((rec_a, rec_b, rec_g, p_rec, back_a, q_back)):
        others(k, ref).wait_send()
    remote(out_b, back_b, ssem.at[6], rsem.at[6], after).wait_send()
    for k in range(7):
        shifts[k].wait_send()
    shifts[6].wait_recv()
    for k, ref in enumerate((got, line, line, got)):
        summed(k, ref).wait_send()


ANY = pl.BlockSpec(memory_space=pl.ANY)
VMEM = pl.BlockSpec(memory_space=pltpu.VMEM)


def like(shape, dtype):
    return jax.ShapeDtypeStruct(shape, dtype)


def body(
    act_in, stash_in, grad_in, route_a, route_b, norm_gain, router, gate_weight, up_weight, down_weight
):
    tokens, width = act_in.shape[1:]
    experts = router.shape[1]
    quarter = gate_weight.shape[2]
    group = lax.axis_size("expert") * lax.axis_size("dp") // ROWS_Z
    slots = experts * MOST
    block = (experts, MOST, width)
    dma = pltpu.SemaphoreType.DMA

    def vb(*shape):
        return pltpu.VMEM(shape, BF16)

    def vf(*shape):
        return pltpu.VMEM(shape, F32)

    full = vb(4, quarter, width)
    row = (tokens, width)
    lanes = (experts, 1, 128)
    next_act, prev_grad, router_grad, gain_grad = pl.pallas_call(
        kernel,
        out_shape=[like(row, BF16), like(row, BF16), like((experts, width), F32), like((1, width), F32)],
        in_specs=[VMEM] * 7 + [ANY] * 3,
        out_specs=[VMEM] * 4,
        scratch_shapes=[vb(*block)] * 6
        + [vb(slots, width)] * 2
        + [full] * 3
        + [vf(slots, width)]
        + [vb(*block)] * 4
        + [vb(*row)] * 2
        + [vb(*row)] * 2
        + [vb(tokens, slots)] * 2
        + [vb(experts, width), vf(1, width)]
        + [vb(tokens, 128)] * 2
        + [vf(slots // 128, 1, 128), vf(*lanes), vf(*lanes), vf(*lanes)]
        + [vf(experts, width), vf(group, ROWS_Z, 8, 128), vf(ROWS_Z, 8, 128)]
        + [vf(group - 1, ROWS_Z, 8, 128), vf(ROWS_Z - 1, 8, 128), vf(group, ROWS_Z, 8, 128)]
        + [dma((7,)), dma((7,)), dma((6,)), dma((7,)), dma((7,))]
        + [dma((3, 3)), dma((3, 3)), dma((3,)), dma((4,)), dma((4,))],
        compiler_params=pltpu.CompilerParams(
            collective_id=0, has_side_effects=True, vmem_limit_bytes=56 << 20
        ),
    )(
        act_in[0], stash_in[0], grad_in[0], route_a[0], route_b[0], norm_gain, router[0],
        gate_weight[0, 0], up_weight[0, 0], down_weight[0, 0],
    )
    return next_act[None], prev_grad[None], router_grad[None], gain_grad


def solution(mesh):
    tokens = P("segment", ("expert", "dp"), None)
    weight = P("segment", "expert", "dp", None)
    router = P("segment", None, None)
    gain = P("segment", None)
    return jax.shard_map(
        body,
        mesh=mesh,
        in_specs=(tokens, tokens, tokens, tokens, tokens, gain, router, weight, weight, weight),
        out_specs=(tokens, tokens, router, gain),
        check_vma=False,
    )
```

time: 333 us -> 300 us (0.901)
  Pallas kernels: 307 us -> 288 us
  matrix products: 16.5 us -> 0 us
    pallas_call x3 -> x1, Pallas kernels: 307 us -> 288 us  [body(): pl.pallas_call(kernel, out_shape=[like(row, BF16), like(row, BF16), like(...]
    dot_general x19 -> x0, matrix products: 16.5 us -> none  [the longest x3 4.49 us: dot_t(): lax.dot_general(a, b, (((1,), (1,)), ((), ())), preferred_element_type=F32)]
    unnamed x28 -> x16, local copies, waits for them, and re-layouts: 1.91 us -> 7.08 us
where the time goes in v2:
time: 300 us; the launch traced here: 296 us
  Pallas kernels  288 us (96%)
  local copies, waits for them, and re-layouts  7.08 us (2%)
    pallas_call x1, Pallas kernels, body(): pl.pallas_call(kernel, out_shape=[like(row, BF16), like(row, BF16), like(...  288 us
    unnamed x16, local copies, waits for them, and re-layouts  7.08 us

profile of v2, /device:TPU:1, one launch (start us, length us, event | category | flops | bytes accessed | tf_op | source)
XLA Modules:
  0.0 296.2 jit_solution(2021859224025950195)
XLA Ops:
  0.6 0.0 copy-start.3
  0.6 0.7 copy-done.3
  1.3 0.7 copy.14
  2.0 0.0 copy-start.4
  2.0 0.7 copy-done.4
  2.7 0.7 copy.15
  3.4 288.5 %shard_map.129 = (bf16[112,2048]{1,0:T(8,128)(2,1)}, bf16[112,2048]{1,0:T(8,128)(2,1)}, f32[32,2048]{1,0:T(8,128)}, f32[1,2048]{1,0:T(1,128)}) custom-call(bf16[112,2048]{1,0:T(8,128)(2,1)} %bitcast.17, bf16[112,2048]{1,0:T(8,128)(2,1)} %bitcast.18, bf16[112,2048]{1,0:T(8,128)(2,1)} %bitcast.19, s32[112,2]{1,0:T(8,128)} %bitcast.21, s32[112,2]{1,0:T(8,128)} %bitcast.22, ...), custom_call_target="tpu_custom_call" | custom-call | tf_op jit(solution)/shard_map/pallas_call | solution.py:432
  291.9 0.0 copy-start
  291.9 1.9 copy.20
  293.8 0.0 copy-done
  293.8 0.0 copy-start.1
  293.8 0.8 copy.21
  294.6 0.3 copy-done.1
  294.9 0.0 copy-start.2
  294.9 0.7 copy.22
  295.6 0.0 copy-done.2
  295.6 0.6 copy.23
Async XLA Ops:
  0.6 0.7 copy-start.3
  2.0 0.7 copy-start.4
  291.9 1.9 copy-start
  293.8 1.1 copy-start.1
  294.9 0.7 copy-start.2

commit v3 on v2

--- a/solution.py
+++ b/solution.py
@@ -112,12 +112,12 @@
 
 
 def kernel(
-    act, stash, grad, route_a, route_b, gain, router, wg, wu, wd,
+    act, stash, grad, routes, gain, router, wg, wu, wd,
     next_act, prev_grad, router_out, gain_out,
     send_a, send_b, send_g, rec_a, rec_b, rec_g, rows, grads, gate, up, down, acc,
     out_a, out_b, back_a, back_b, normed_b, mixed,
     stash_s, grad_s, picks_b, picks_s, router_s, gain_s, dlog, dlog_s,
-    p_send, p_rec, q_send, q_back, rsum, term, held, got, line, total,
+    p_send, p_rec, q_send, q_back, rsum, wide, term, held, got, line, total,
     ssem, rsem, own, shift_send, shift_recv, wsend, wrecv, wown, sum_send, sum_recv,
 ):
     me = Place()
@@ -199,11 +199,13 @@
             device, expert, slot = me.owner(j)
             remote(src.at[block(expert)], dst.at[slot], ssem.at[k], rsem.at[k], device).start()
 
-    def send_back(k, src, dst):
-        expert = me.expert()
+    expert = me.expert()
+
+    def keep_back(k, src, dst):
         pltpu.make_async_copy(src.at[me.client(0)[1]], dst.at[expert], own.at[k]).start()
 
-        @pl.loop(1, count)
+    def send_back(k, src, dst, first, last):
+        @pl.loop(first, last)
         def _(j):
             device, slot = me.client(j)
             remote(src.at[slot], dst.at[expert], ssem.at[k], rsem.at[k], device).start()
@@ -221,13 +223,11 @@
         to_core(m).start()
         to_self(m).start()
     gain_row = gain[...]
-    normed_a, weights_a, picks_a = prepare(act[...], route_a[...], gain_row, router[...])
+    normed_a, weights_a, picks_a = prepare(act[...], routes[:, 0:2], gain_row, router[...])
     send_a[...] = to_slots((picks_a[0] + picks_a[1]).astype(BF16), normed_a)
     send(0, send_a, rec_a)
-    for k in range(4):
-        shifts[k].start()
-
-    normed, weights_b, picks = prepare(stash[...], route_b[...], gain_row, router[...])
+
+    normed, weights_b, picks = prepare(stash[...], routes[:, 2:4], gain_row, router[...])
     normed_b[...] = normed
     both = (picks[0] + picks[1]).astype(BF16)
     picks_b[...] = both
@@ -236,6 +236,8 @@
     send(1, send_b, rec_b)
     send_g[...] = to_slots(both, grad[...])
     send(2, send_g, rec_g)
+    for k in range(4):
+        shifts[k].start()
     p_row = jnp.sum(picks[0] * weights_b[0] + picks[1] * weights_b[1], 0, keepdims=True)
     halves = p_send.shape[0]
     for h in range(halves):
@@ -262,10 +264,12 @@
         acc[...] += dot(hidden, down[c])
 
     out_a[...] = acc[...].reshape(out_a.shape).astype(BF16)
+    keep_back(4, out_a, back_a)
+    send_back(4, out_a, back_a, 1, count // 2)
     arrived(1, rec_b)
     arrived(2, rec_g)
     arrived(3, p_rec)
-    send_back(4, out_a, back_a)
+    send_back(4, out_a, back_a, count // 2, count)
 
     rows[...] = flat(rec_b[...])
     grads[...] = flat(rec_g[...])
@@ -288,18 +292,20 @@
     base = (me.expert() % per_half) * MOST
     lanes = ones(iota((count, MOST, 128), 2) == iota((count, MOST, 128), 1) + base)
     q_send[...] = jnp.sum(lanes * dots.reshape(count, MOST, 1), 1, keepdims=True)
-    send_back(5, q_send, q_back)
+    keep_back(5, q_send, q_back)
+    send_back(5, q_send, q_back, 1, count)
     p_col = jnp.sum(lanes * p_rec[...], 2, keepdims=True).reshape(slots, 1)
     scaled = acc[...] * p_col
     out_b[...] = scaled.reshape(out_b.shape).astype(BF16)
-    expert = me.expert()
-
-    @pl.loop(0, count)
-    def _(j):
-        device, slot = me.client(j)
-        device = (behind, device[1], device[2])
-        remote(out_b.at[slot], back_b.at[expert], ssem.at[6], rsem.at[6], device).start()
-
+
+    def grads_back(part):
+        @pl.loop(part * count // 4, (part + 1) * count // 4)
+        def _(j):
+            device, slot = me.client(j)
+            device = (behind, device[1], device[2])
+            remote(out_b.at[slot], back_b.at[expert], ssem.at[6], rsem.at[6], device).start()
+
+    grads_back(0)
     gain_own = jnp.sum(scaled * rows[...].astype(F32), 0, keepdims=True) / gain_row
 
     arrived(5, q_back)
@@ -310,8 +316,7 @@
     dot_of = [jnp.sum(pick * q_row, -1, keepdims=True) for pick in picks]
     logit_grad = weights_b[0] * weights_b[1] * (dot_of[0] - dot_of[1])
     ids = iota((tokens, 128), 1)
-    route = route_b[...]
-    signs = ones(route[:, 0:1] == ids) - ones(route[:, 1:2] == ids)
+    signs = ones(routes[:, 2:3] == ids) - ones(routes[:, 3:4] == ids)
     dlogits = (logit_grad * signs).astype(BF16)
     dlog[...] = dlogits
     shifts[5].start()
@@ -320,12 +325,13 @@
     rsum[...] = dot(dlogits, normed_b[...], ((0,), (0,)))
     gain_part = gain_own + jnp.sum(dot(dlogits, router[...]) * x_float * inv_rms, 0, keepdims=True)
     per = count // group
-    term[...] = jnp.zeros_like(term)
+    wide[...] = jnp.zeros_like(wide)
     for g in range(group):
         for c in range(ROWS_Z):
-            term[g, c, 0:per, :] = rsum[g * per : (g + 1) * per, c * 128 : (c + 1) * 128]
+            wide[g, c, 0:per, :] = rsum[g * per : (g + 1) * per, c * 128 : (c + 1) * 128]
     for c in range(ROWS_Z):
-        term[0, c, per : per + 1, :] = gain_part[:, c * 128 : (c + 1) * 128]
+        wide[0, c, per : per + 1, :] = gain_part[:, c * 128 : (c + 1) * 128]
+    term[...] = wide[...].astype(BF16)
 
     @pl.loop(1, group)
     def _(o):
@@ -335,22 +341,25 @@
     def summed(k, ref):
         return remote(ref, ref, sum_send.at[k], sum_recv.at[k], after)
 
+    grads_back(1)
     summed(0, got).wait_recv()
-    held[...] = term[mine] + jnp.sum(got[...], 0)
+    held[...] = (wide[mine] + jnp.sum(got[...].astype(F32), 0)).astype(BF16)
 
     @pl.loop(1, ROWS_Z)
     def _(o):
         other, device = in_column(o)
         remote(held.at[other], line.at[o - 1], sum_send.at[1], sum_recv.at[1], device).start()
 
+    grads_back(2)
     summed(1, line).wait_recv()
-    total[mine, me.z] = held[me.z] + jnp.sum(line[...], 0)
+    total[mine, me.z] = (held[me.z].astype(F32) + jnp.sum(line[...].astype(F32), 0)).astype(BF16)
 
     @pl.loop(1, ROWS_Z)
     def _(o):
         here = total.at[mine, me.z]
         remote(here, here, sum_send.at[2], sum_recv.at[2], in_column(o)[1]).start()
 
+    grads_back(3)
     summed(2, line).wait_recv()
 
     @pl.loop(1, group)
@@ -368,11 +377,12 @@
 
     summed(3, got).wait_recv()
     scale = 1.0 / (group * ROWS_Z)
+    wide[...] = total[...].astype(F32) * scale
     for g in range(group):
         for c in range(ROWS_Z):
-            router_out[g * per : (g + 1) * per, c * 128 : (c + 1) * 128] = total[g, c, 0:per, :] * scale
+            router_out[g * per : (g + 1) * per, c * 128 : (c + 1) * 128] = wide[g, c, 0:per, :]
     for c in range(ROWS_Z):
-        gain_out[:, c * 128 : (c + 1) * 128] = total[0, c, per : per + 1, :] * scale
+        gain_out[:, c * 128 : (c + 1) * 128] = wide[0, c, per : per + 1, :]
 
     for k in range(6):
         shifts[k].wait_recv()
@@ -432,7 +442,7 @@
     next_act, prev_grad, router_grad, gain_grad = pl.pallas_call(
         kernel,
         out_shape=[like(row, BF16), like(row, BF16), like((experts, width), F32), like((1, width), F32)],
-        in_specs=[VMEM] * 7 + [ANY] * 3,
+        in_specs=[VMEM] * 6 + [ANY] * 3,
         out_specs=[VMEM] * 4,
         scratch_shapes=[vb(*block)] * 6
         + [vb(slots, width)] * 2
@@ -445,15 +455,15 @@
         + [vb(experts, width), vf(1, width)]
         + [vb(tokens, 128)] * 2
         + [vf(slots // 128, 1, 128), vf(*lanes), vf(*lanes), vf(*lanes)]
-        + [vf(experts, width), vf(group, ROWS_Z, 8, 128), vf(ROWS_Z, 8, 128)]
-        + [vf(group - 1, ROWS_Z, 8, 128), vf(ROWS_Z - 1, 8, 128), vf(group, ROWS_Z, 8, 128)]
+        + [vf(experts, width), vf(group, ROWS_Z, 8, 128), vb(group, ROWS_Z, 8, 128), vb(ROWS_Z, 8, 128)]
+        + [vb(group - 1, ROWS_Z, 8, 128), vb(ROWS_Z - 1, 8, 128), vb(group, ROWS_Z, 8, 128)]
         + [dma((7,)), dma((7,)), dma((6,)), dma((7,)), dma((7,))]
         + [dma((3, 3)), dma((3, 3)), dma((3,)), dma((4,)), dma((4,))],
         compiler_params=pltpu.CompilerParams(
             collective_id=0, has_side_effects=True, vmem_limit_bytes=56 << 20
         ),
     )(
-        act_in[0], stash_in[0], grad_in[0], route_a[0], route_b[0], norm_gain, router[0],
+        act_in[0], stash_in[0], grad_in[0], jnp.concatenate([route_a[0], route_b[0]], 1), norm_gain, router[0],
         gate_weight[0, 0], up_weight[0, 0], down_weight[0, 0],
     )
     return next_act[None], prev_grad[None], router_grad[None], gain_grad

time: 300 us -> 275 us (0.917); the launches traced: 296 us -> 274 us
  Pallas kernels: 288 us -> 268 us
    pallas_call x1, Pallas kernels: 288 us -> 268 us  [body(): pl.pallas_call(kernel, out_shape=[like(row, BF16), like(row, BF16), like(...]
    unnamed x16 -> x14, local copies, waits for them, and re-layouts: 7.08 us -> 4.95 us
where the time goes in v3:
time: 275 us; the launch traced here: 274 us
  Pallas kernels  268 us (97%)
  local copies, waits for them, and re-layouts  5.69 us (2%)
    pallas_call x1, Pallas kernels, body(): pl.pallas_call(kernel, out_shape=[like(row, BF16), like(row, BF16), like(...  268 us

profile of v3, /device:TPU:1, one launch (start us, length us, event | category | flops | bytes accessed | tf_op | source)
XLA Modules:
  0.0 274.5 jit_solution(15702984019978639715)
XLA Ops:
  0.6 0.0 copy-start.4
  0.6 0.0 copy-start.3
  0.7 0.7 copy-done.4
  1.3 0.0 copy-done.3
  1.3 0.7 copy.16.routes
  2.1 268.1 %shard_map.129 = (bf16[112,2048]{1,0:T(8,128)(2,1)}, bf16[112,2048]{1,0:T(8,128)(2,1)}, f32[32,2048]{1,0:T(8,128)}, f32[1,2048]{1,0:T(1,128)}) custom-call(bf16[112,2048]{1,0:T(8,128)(2,1)} %bitcast.15, bf16[112,2048]{1,0:T(8,128)(2,1)} %bitcast.16, bf16[112,2048]{1,0:T(8,128)(2,1)} %bitcast.17, s32[112,4]{1,0:T(8,128)} %copy.16.routes, f32[1,2048]{1,0:T(1,128)} %gain.1, ...), custom_call_target="tpu_custom_call" | custom-call | tf_op jit(solution)/shard_map/pallas_call | solution.py:442
  270.2 0.0 copy-start
  270.2 1.9 copy.21
  272.1 0.0 copy-done
  272.1 0.0 copy-start.1
  272.1 0.8 copy.22
  272.8 0.3 copy-done.1
  273.2 0.0 copy-start.2
  273.2 0.7 copy.23
  273.9 0.0 copy-done.2
  273.9 0.6 copy.24
  (1 shorter events, 0.0 us)
Async XLA Ops:
  0.6 0.7 copy-start.4
  0.6 0.7 copy-start.3
  270.2 1.9 copy-start
  272.1 1.1 copy-start.1
  273.2 0.7 copy-start.2

commit v4 on v3

--- a/solution.py
+++ b/solution.py
@@ -82,6 +82,13 @@
     return x_float, inv_rms
 
 
+def columns(route):
+    tokens = route.shape[1]
+    same = ones(iota((tokens, tokens), 0) == iota((tokens, tokens), 1))
+    values = route.astype(F32)
+    return [jnp.sum(same * values[k : k + 1, :], -1, keepdims=True).astype(jnp.int32) for k in range(2)]
+
+
 def prepare(x, route, gain, router_w):
     tokens = x.shape[0]
     experts = router_w.shape[0]
@@ -89,7 +96,7 @@
     normed = (x_float * inv_rms * gain).astype(BF16)
     logits = dot_t(normed, router_w)
     ids = iota((tokens, experts), 1)
-    hot = [ones(route[:, k : k + 1] == ids) for k in range(2)]
+    hot = [ones(route[k] == ids) for k in range(2)]
     chosen = [jnp.sum(h * logits, -1, keepdims=True) for h in hot]
     weights = (jax.nn.sigmoid(chosen[0] - chosen[1]), jax.nn.sigmoid(chosen[1] - chosen[0]))
     below = ones(iota((tokens, tokens), 0) > iota((tokens, tokens), 1)).astype(BF16)
@@ -98,7 +105,7 @@
     picks = []
     for k in range(2):
         rank = jnp.sum(hot[k] * counts, -1, keepdims=True).astype(jnp.int32)
-        picks.append(ones(route[:, k : k + 1] * MOST + rank == slots))
+        picks.append(ones(route[k] * MOST + rank == slots))
     return normed, weights, picks
 
 
@@ -112,7 +119,7 @@
 
 
 def kernel(
-    act, stash, grad, routes, gain, router, wg, wu, wd,
+    act, stash, grad, route_a, route_b, gain, router, wg, wu, wd,
     next_act, prev_grad, router_out, gain_out,
     send_a, send_b, send_g, rec_a, rec_b, rec_g, rows, grads, gate, up, down, acc,
     out_a, out_b, back_a, back_b, normed_b, mixed,
@@ -160,6 +167,21 @@
     def _(o):
         signal(barrier, in_column(o)[1])
 
+    gain_row = gain[...]
+    normed_a, weights_a, picks_a = prepare(act[...], columns(route_a[...]), gain_row, router[...])
+    send_a[...] = to_slots((picks_a[0] + picks_a[1]).astype(BF16), normed_a)
+    route_cols = columns(route_b[...])
+    normed, weights_b, picks = prepare(stash[...], route_cols, gain_row, router[...])
+    normed_b[...] = normed
+    both = (picks[0] + picks[1]).astype(BF16)
+    picks_b[...] = both
+    send_b[...] = to_slots(both, normed)
+    send_g[...] = to_slots(both, grad[...])
+    p_row = jnp.sum(picks[0] * weights_b[0] + picks[1] * weights_b[1], 0, keepdims=True)
+    halves = p_send.shape[0]
+    for h in range(halves):
+        p_send[h] = p_row[:, h * 128 : (h + 1) * 128]
+    per_half = count // halves
     pl.semaphore_wait(barrier, 4 + 3 * (count - 1) + group - 1 + ROWS_Z - 1)
 
     weights = ((wg, gate), (wu, up), (wd, down))
@@ -222,28 +244,12 @@
         to_twin(m).start()
         to_core(m).start()
         to_self(m).start()
-    gain_row = gain[...]
-    normed_a, weights_a, picks_a = prepare(act[...], routes[:, 0:2], gain_row, router[...])
-    send_a[...] = to_slots((picks_a[0] + picks_a[1]).astype(BF16), normed_a)
     send(0, send_a, rec_a)
-
-    normed, weights_b, picks = prepare(stash[...], routes[:, 2:4], gain_row, router[...])
-    normed_b[...] = normed
-    both = (picks[0] + picks[1]).astype(BF16)
-    picks_b[...] = both
-    shifts[4].start()
-    send_b[...] = to_slots(both, normed)
     send(1, send_b, rec_b)
-    send_g[...] = to_slots(both, grad[...])
     send(2, send_g, rec_g)
-    for k in range(4):
+    send(3, p_send, p_rec, lambda e: e // per_half)
+    for k in range(5):
         shifts[k].start()
-    p_row = jnp.sum(picks[0] * weights_b[0] + picks[1] * weights_b[1], 0, keepdims=True)
-    halves = p_send.shape[0]
-    for h in range(halves):
-        p_send[h] = p_row[:, h * 128 : (h + 1) * 128]
-    per_half = count // halves
-    send(3, p_send, p_rec, lambda e: e // per_half)
 
     for m in range(3):
         to_twin(m).wait_recv()
@@ -299,7 +305,9 @@
     out_b[...] = scaled.reshape(out_b.shape).astype(BF16)
 
     def grads_back(part):
-        @pl.loop(part * count // 4, (part + 1) * count // 4)
+        cuts = (0, 12, 20, 28, count)
+
+        @pl.loop(cuts[part], cuts[part + 1])
         def _(j):
             device, slot = me.client(j)
             device = (behind, device[1], device[2])
@@ -316,7 +324,7 @@
     dot_of = [jnp.sum(pick * q_row, -1, keepdims=True) for pick in picks]
     logit_grad = weights_b[0] * weights_b[1] * (dot_of[0] - dot_of[1])
     ids = iota((tokens, 128), 1)
-    signs = ones(routes[:, 2:3] == ids) - ones(routes[:, 3:4] == ids)
+    signs = ones(route_cols[0] == ids) - ones(route_cols[1] == ids)
     dlogits = (logit_grad * signs).astype(BF16)
     dlog[...] = dlogits
     shifts[5].start()
@@ -411,7 +419,7 @@
         summed(k, ref).wait_send()
 
 
-ANY = pl.BlockSpec(memory_space=pl.ANY)
+HBM = pl.BlockSpec(memory_space=pltpu.HBM)
 VMEM = pl.BlockSpec(memory_space=pltpu.VMEM)
 
 
@@ -442,7 +450,7 @@
     next_act, prev_grad, router_grad, gain_grad = pl.pallas_call(
         kernel,
         out_shape=[like(row, BF16), like(row, BF16), like((experts, width), F32), like((1, width), F32)],
-        in_specs=[VMEM] * 6 + [ANY] * 3,
+        in_specs=[VMEM] * 7 + [HBM] * 3,
         out_specs=[VMEM] * 4,
         scratch_shapes=[vb(*block)] * 6
         + [vb(slots, width)] * 2
@@ -460,10 +468,10 @@
         + [dma((7,)), dma((7,)), dma((6,)), dma((7,)), dma((7,))]
         + [dma((3, 3)), dma((3, 3)), dma((3,)), dma((4,)), dma((4,))],
         compiler_params=pltpu.CompilerParams(
-            collective_id=0, has_side_effects=True, vmem_limit_bytes=56 << 20
+            collective_id=0, has_side_effects=True, vmem_limit_bytes=40 << 20
         ),
     )(
-        act_in[0], stash_in[0], grad_in[0], jnp.concatenate([route_a[0], route_b[0]], 1), norm_gain, router[0],
+        act_in[0], stash_in[0], grad_in[0], route_a[0].T, route_b[0].T, norm_gain, router[0],
         gate_weight[0, 0], up_weight[0, 0], down_weight[0, 0],
     )
     return next_act[None], prev_grad[None], router_grad[None], gain_grad

time: 275 us -> 283 us (1.029)
  local copies, waits for them, and re-layouts: 5.69 us -> 10.8 us
  Pallas kernels: 268 us -> 271 us
    unnamed x14 -> x24, local copies, waits for them, and re-layouts: 4.95 us -> 10.8 us
    pallas_call x1, Pallas kernels: 268 us -> 271 us  [body(): pl.pallas_call(kernel, out_shape=[like(row, BF16), like(row, BF16), like(...]
where the time goes in v4:
time: 283 us
  Pallas kernels  271 us (96%)
  local copies, waits for them, and re-layouts  10.8 us (4%)
    pallas_call x1, Pallas kernels, body(): pl.pallas_call(kernel, out_shape=[like(row, BF16), like(row, BF16), like(...  271 us
    unnamed x24, local copies, waits for them, and re-layouts  10.8 us

profile of v4, /device:TPU:1, one launch (start us, length us, event | category | flops | bytes accessed | tf_op | source)
XLA Modules:
  0.0 282.8 jit_solution(7690947022456432166)
XLA Ops:
  0.6 0.0 copy-start.7
  0.6 0.0 copy-start.9
  0.7 0.0 copy-start.8
  0.7 0.7 copy-done.7
  1.3 0.0 copy-done.9
  1.3 0.0 copy-done.8
  1.3 0.0 copy-start
  1.3 1.1 copy-done
  2.5 0.0 copy-start.1
  2.5 1.1 copy-done.1
  3.6 0.0 copy-start.2
  3.6 1.1 copy-done.2
  4.7 0.0 copy-start.3
  4.7 1.0 copy-done.3
  5.7 0.0 copy-start.4
  5.7 1.0 copy-done.4
  6.7 0.0 copy-start.5
  6.7 1.0 copy-done.5
  7.7 0.0 copy-start.6
  7.7 0.9 copy-done.6
  8.6 271.4 %shard_map.129 = (bf16[112,2048]{1,0:T(8,128)(2,1)S(1)}, bf16[112,2048]{1,0:T(8,128)(2,1)S(1)}, f32[32,2048]{1,0:T(8,128)S(1)}, f32[1,2048]{1,0:T(1,128)S(1)}) custom-call(bf16[112,2048]{1,0:T(8,128)(2,1)S(1)} %bitcast.19, bf16[112,2048]{1,0:T(8,128)(2,1)S(1)} %bitcast.20, bf16[112,2048]{1,0:T(8,128)(2,1)S(1)} %bitcast.21, s32[2,112]{1,0:T(2,128)S(1)} %bitcast.26, ...), custom_call_target="tpu_custom_call" | custom-call | tf_op jit(solution)/shard_map/pallas_call | solution.py:450
  280.0 0.8 copy.18
  280.8 0.8 copy.19
  281.5 0.7 copy.20
  282.2 0.6 copy.21
Async XLA Ops:
  0.6 0.7 copy-start.7
  0.6 0.7 copy-start.9
  0.7 0.7 copy-start.8
  1.3 1.1 copy-start
  2.5 1.1 copy-start.1
  3.6 1.1 copy-start.2
  4.7 1.0 copy-start.3
  5.7 1.0 copy-start.4
  6.7 1.0 copy-start.5
  7.7 0.9 copy-start.6

commit v5 on v3

--- a/solution.py
+++ b/solution.py
@@ -82,24 +82,33 @@
     return x_float, inv_rms
 
 
-def prepare(x, route, gain, router_w):
-    tokens = x.shape[0]
-    experts = router_w.shape[0]
-    x_float, inv_rms = norm_of(x)
-    normed = (x_float * inv_rms * gain).astype(BF16)
-    logits = dot_t(normed, router_w)
+def columns(route):
+    tokens = route.shape[1]
+    same = ones(iota((tokens, tokens), 0) == iota((tokens, tokens), 1))
+    values = route.astype(F32)
+    return [jnp.sum(same * values[k : k + 1, :], -1, keepdims=True).astype(jnp.int32) for k in range(2)]
+
+
+def choose(route, experts):
+    tokens = route[0].shape[0]
     ids = iota((tokens, experts), 1)
-    hot = [ones(route[:, k : k + 1] == ids) for k in range(2)]
-    chosen = [jnp.sum(h * logits, -1, keepdims=True) for h in hot]
-    weights = (jax.nn.sigmoid(chosen[0] - chosen[1]), jax.nn.sigmoid(chosen[1] - chosen[0]))
+    hot = [ones(r == ids) for r in route]
     below = ones(iota((tokens, tokens), 0) > iota((tokens, tokens), 1)).astype(BF16)
     counts = dot(below, (hot[0] + hot[1]).astype(BF16))
     slots = iota((tokens, experts * MOST), 1)
     picks = []
     for k in range(2):
         rank = jnp.sum(hot[k] * counts, -1, keepdims=True).astype(jnp.int32)
-        picks.append(ones(route[:, k : k + 1] * MOST + rank == slots))
-    return normed, weights, picks
+        picks.append(ones(route[k] * MOST + rank == slots))
+    return hot, picks
+
+
+def prepare(x, hot, gain, router_w):
+    x_float, inv_rms = norm_of(x)
+    normed = (x_float * inv_rms * gain).astype(BF16)
+    logits = dot_t(normed, router_w)
+    chosen = [jnp.sum(h * logits, -1, keepdims=True) for h in hot]
+    return normed, (jax.nn.sigmoid(chosen[0] - chosen[1]), jax.nn.sigmoid(chosen[1] - chosen[0]))
 
 
 def to_slots(both, rows):
@@ -112,7 +121,7 @@
 
 
 def kernel(
-    act, stash, grad, routes, gain, router, wg, wu, wd,
+    act, stash, grad, route_a, route_b, gain, router, wg, wu, wd,
     next_act, prev_grad, router_out, gain_out,
     send_a, send_b, send_g, rec_a, rec_b, rec_g, rows, grads, gate, up, down, acc,
     out_a, out_b, back_a, back_b, normed_b, mixed,
@@ -223,20 +232,21 @@
         to_core(m).start()
         to_self(m).start()
     gain_row = gain[...]
-    normed_a, weights_a, picks_a = prepare(act[...], routes[:, 0:2], gain_row, router[...])
+    route_cols = columns(route_b[...])
+    hot, picks = choose(route_cols, count)
+    both = (picks[0] + picks[1]).astype(BF16)
+    send_g[...] = to_slots(both, grad[...])
+    send(2, send_g, rec_g)
+    normed, weights_b = prepare(stash[...], hot, gain_row, router[...])
+    send_b[...] = to_slots(both, normed)
+    send(1, send_b, rec_b)
+    hot_a, picks_a = choose(columns(route_a[...]), count)
+    normed_a, weights_a = prepare(act[...], hot_a, gain_row, router[...])
     send_a[...] = to_slots((picks_a[0] + picks_a[1]).astype(BF16), normed_a)
     send(0, send_a, rec_a)
-
-    normed, weights_b, picks = prepare(stash[...], routes[:, 2:4], gain_row, router[...])
     normed_b[...] = normed
-    both = (picks[0] + picks[1]).astype(BF16)
     picks_b[...] = both
-    shifts[4].start()
-    send_b[...] = to_slots(both, normed)
-    send(1, send_b, rec_b)
-    send_g[...] = to_slots(both, grad[...])
-    send(2, send_g, rec_g)
-    for k in range(4):
+    for k in range(5):
         shifts[k].start()
     p_row = jnp.sum(picks[0] * weights_b[0] + picks[1] * weights_b[1], 0, keepdims=True)
     halves = p_send.shape[0]
@@ -265,11 +275,11 @@
 
     out_a[...] = acc[...].reshape(out_a.shape).astype(BF16)
     keep_back(4, out_a, back_a)
-    send_back(4, out_a, back_a, 1, count // 2)
+    send_back(4, out_a, back_a, 1, count * 5 // 8)
     arrived(1, rec_b)
     arrived(2, rec_g)
     arrived(3, p_rec)
-    send_back(4, out_a, back_a, count // 2, count)
+    send_back(4, out_a, back_a, count * 5 // 8, count)
 
     rows[...] = flat(rec_b[...])
     grads[...] = flat(rec_g[...])
@@ -316,7 +326,7 @@
     dot_of = [jnp.sum(pick * q_row, -1, keepdims=True) for pick in picks]
     logit_grad = weights_b[0] * weights_b[1] * (dot_of[0] - dot_of[1])
     ids = iota((tokens, 128), 1)
-    signs = ones(routes[:, 2:3] == ids) - ones(routes[:, 3:4] == ids)
+    signs = ones(route_cols[0] == ids) - ones(route_cols[1] == ids)
     dlogits = (logit_grad * signs).astype(BF16)
     dlog[...] = dlogits
     shifts[5].start()
@@ -442,7 +452,7 @@
     next_act, prev_grad, router_grad, gain_grad = pl.pallas_call(
         kernel,
         out_shape=[like(row, BF16), like(row, BF16), like((experts, width), F32), like((1, width), F32)],
-        in_specs=[VMEM] * 6 + [ANY] * 3,
+        in_specs=[VMEM] * 7 + [ANY] * 3,
         out_specs=[VMEM] * 4,
         scratch_shapes=[vb(*block)] * 6
         + [vb(slots, width)] * 2
@@ -463,7 +473,7 @@
             collective_id=0, has_side_effects=True, vmem_limit_bytes=56 << 20
         ),
     )(
-        act_in[0], stash_in[0], grad_in[0], jnp.concatenate([route_a[0], route_b[0]], 1), norm_gain, router[0],
+        act_in[0], stash_in[0], grad_in[0], route_a[0].T, route_b[0].T, norm_gain, router[0],
         gate_weight[0, 0], up_weight[0, 0], down_weight[0, 0],
     )
     return next_act[None], prev_grad[None], router_grad[None], gain_grad

time: 275 us -> 281 us (1.022)
  Pallas kernels: 268 us -> 275 us
    pallas_call x1, Pallas kernels: 268 us -> 275 us  [body(): pl.pallas_call(kernel, out_shape=[like(row, BF16), like(row, BF16), like(...]
where the time goes in v5:
time: 281 us; the launch traced here: 279 us
  Pallas kernels  275 us (98%)
  local copies, waits for them, and re-layouts  4.27 us (2%)
    pallas_call x1, Pallas kernels, body(): pl.pallas_call(kernel, out_shape=[like(row, BF16), like(row, BF16), like(...  275 us

profile of v5, /device:TPU:1, one launch (start us, length us, event | category | flops | bytes accessed | tf_op | source)
XLA Modules:
  0.0 279.5 jit_solution(1096554880843540450)
XLA Ops:
  0.6 274.6 %shard_map.129 = (bf16[112,2048]{1,0:T(8,128)(2,1)}, bf16[112,2048]{1,0:T(8,128)(2,1)}, f32[32,2048]{1,0:T(8,128)}, f32[1,2048]{1,0:T(1,128)}) custom-call(bf16[112,2048]{1,0:T(8,128)(2,1)} %bitcast.19, bf16[112,2048]{1,0:T(8,128)(2,1)} %bitcast.20, bf16[112,2048]{1,0:T(8,128)(2,1)} %bitcast.21, s32[2,112]{1,0:T(2,128)} %bitcast.26, s32[2,112]{1,0:T(2,128)} %bitcast.27, ...), custom_call_target="tpu_custom_call" | custom-call | tf_op jit(solution)/shard_map/pallas_call | solution.py:452
  275.2 0.0 copy-start
  275.2 1.9 copy.18
  277.1 0.0 copy-done
  277.1 0.0 copy-start.1
  277.1 0.8 copy.19
  277.9 0.3 copy-done.1
  278.2 0.0 copy-start.2
  278.2 0.7 copy.20
  278.9 0.0 copy-done.2
  278.9 0.6 copy.21
Async XLA Ops:
  275.2 1.9 copy-start
  277.1 1.1 copy-start.1
  278.2 0.7 copy-start.2

commit v6 on v3

--- a/solution.py
+++ b/solution.py
@@ -82,6 +82,13 @@
     return x_float, inv_rms
 
 
+def columns(route):
+    tokens = route.shape[1]
+    same = ones(iota((tokens, tokens), 0) == iota((tokens, tokens), 1))
+    values = route.astype(F32)
+    return [jnp.sum(same * values[k : k + 1, :], -1, keepdims=True).astype(jnp.int32) for k in range(2)]
+
+
 def prepare(x, route, gain, router_w):
     tokens = x.shape[0]
     experts = router_w.shape[0]
@@ -89,7 +96,7 @@
     normed = (x_float * inv_rms * gain).astype(BF16)
     logits = dot_t(normed, router_w)
     ids = iota((tokens, experts), 1)
-    hot = [ones(route[:, k : k + 1] == ids) for k in range(2)]
+    hot = [ones(route[k] == ids) for k in range(2)]
     chosen = [jnp.sum(h * logits, -1, keepdims=True) for h in hot]
     weights = (jax.nn.sigmoid(chosen[0] - chosen[1]), jax.nn.sigmoid(chosen[1] - chosen[0]))
     below = ones(iota((tokens, tokens), 0) > iota((tokens, tokens), 1)).astype(BF16)
@@ -98,7 +105,7 @@
     picks = []
     for k in range(2):
         rank = jnp.sum(hot[k] * counts, -1, keepdims=True).astype(jnp.int32)
-        picks.append(ones(route[:, k : k + 1] * MOST + rank == slots))
+        picks.append(ones(route[k] * MOST + rank == slots))
     return normed, weights, picks
 
 
@@ -112,7 +119,7 @@
 
 
 def kernel(
-    act, stash, grad, routes, gain, router, wg, wu, wd,
+    act, stash, grad, route_a, route_b, gain, router, wg, wu, wd,
     next_act, prev_grad, router_out, gain_out,
     send_a, send_b, send_g, rec_a, rec_b, rec_g, rows, grads, gate, up, down, acc,
     out_a, out_b, back_a, back_b, normed_b, mixed,
@@ -223,11 +230,12 @@
         to_core(m).start()
         to_self(m).start()
     gain_row = gain[...]
-    normed_a, weights_a, picks_a = prepare(act[...], routes[:, 0:2], gain_row, router[...])
+    normed_a, weights_a, picks_a = prepare(act[...], columns(route_a[...]), gain_row, router[...])
     send_a[...] = to_slots((picks_a[0] + picks_a[1]).astype(BF16), normed_a)
     send(0, send_a, rec_a)
 
-    normed, weights_b, picks = prepare(stash[...], routes[:, 2:4], gain_row, router[...])
+    route_cols = columns(route_b[...])
+    normed, weights_b, picks = prepare(stash[...], route_cols, gain_row, router[...])
     normed_b[...] = normed
     both = (picks[0] + picks[1]).astype(BF16)
     picks_b[...] = both
@@ -316,7 +324,7 @@
     dot_of = [jnp.sum(pick * q_row, -1, keepdims=True) for pick in picks]
     logit_grad = weights_b[0] * weights_b[1] * (dot_of[0] - dot_of[1])
     ids = iota((tokens, 128), 1)
-    signs = ones(routes[:, 2:3] == ids) - ones(routes[:, 3:4] == ids)
+    signs = ones(route_cols[0] == ids) - ones(route_cols[1] == ids)
     dlogits = (logit_grad * signs).astype(BF16)
     dlog[...] = dlogits
     shifts[5].start()
@@ -442,7 +450,7 @@
     next_act, prev_grad, router_grad, gain_grad = pl.pallas_call(
         kernel,
         out_shape=[like(row, BF16), like(row, BF16), like((experts, width), F32), like((1, width), F32)],
-        in_specs=[VMEM] * 6 + [ANY] * 3,
+        in_specs=[VMEM] * 7 + [ANY] * 3,
         out_specs=[VMEM] * 4,
         scratch_shapes=[vb(*block)] * 6
         + [vb(slots, width)] * 2
@@ -463,7 +471,7 @@
             collective_id=0, has_side_effects=True, vmem_limit_bytes=56 << 20
         ),
     )(
-        act_in[0], stash_in[0], grad_in[0], jnp.concatenate([route_a[0], route_b[0]], 1), norm_gain, router[0],
+        act_in[0], stash_in[0], grad_in[0], route_a[0].T, route_b[0].T, norm_gain, router[0],
         gate_weight[0, 0], up_weight[0, 0], down_weight[0, 0],
     )
     return next_act[None], prev_grad[None], router_grad[None], gain_grad

time: 275 us -> 273 us (level)
  no operation moved by 1% of the time
where the time goes in v6:
time: 273 us
  Pallas kernels  268 us (98%)
  local copies, waits for them, and re-layouts  4.27 us (2%)
    pallas_call x1, Pallas kernels, body(): pl.pallas_call(kernel, out_shape=[like(row, BF16), like(row, BF16), like(...  268 us

profile of v6, /device:TPU:1, one launch (start us, length us, event | category | flops | bytes accessed | tf_op | source)
XLA Modules:
  0.0 273.1 jit_solution(4655338645157530157)
XLA Ops:
  0.6 268.2 %shard_map.129 = (bf16[112,2048]{1,0:T(8,128)(2,1)}, bf16[112,2048]{1,0:T(8,128)(2,1)}, f32[32,2048]{1,0:T(8,128)}, f32[1,2048]{1,0:T(1,128)}) custom-call(bf16[112,2048]{1,0:T(8,128)(2,1)} %bitcast.19, bf16[112,2048]{1,0:T(8,128)(2,1)} %bitcast.20, bf16[112,2048]{1,0:T(8,128)(2,1)} %bitcast.21, s32[2,112]{1,0:T(2,128)} %bitcast.26, s32[2,112]{1,0:T(2,128)} %bitcast.27, ...), custom_call_target="tpu_custom_call" | custom-call | tf_op jit(solution)/shard_map/pallas_call | solution.py:450
  268.8 0.0 copy-start
  268.9 1.9 copy.18
  270.7 0.0 copy-done
  270.7 0.0 copy-start.1
  270.7 0.8 copy.19
  271.5 0.3 copy-done.1
  271.8 0.0 copy-start.2
  271.8 0.7 copy.20
  272.5 0.0 copy-done.2
  272.5 0.6 copy.21
Async XLA Ops:
  268.8 1.9 copy-start
  270.7 1.1 copy-start.1
  271.8 0.7 copy-start.2
